TPU v7x, 128 devices: a whole 4x4x4 slice. The times are simulated.
128 devices in a mesh: ctx: 8 (over x, z_hi), frame: 16 (over z_lo, y, core).
Axes of the slice: x: 4, y: 4, z: 4 (z_hi: 2, z_lo: 2; z = z_hi * 2 + z_lo), core: 2. Of those that a mesh axis runs over, the one named last changes fastest.
Arguments:
- queries: bfloat16 [4096, 4096], P('ctx', 'frame'), may hold values from -160 to 160
- keys: bfloat16 [8192, 4096], P('ctx', 'frame'), may hold values from -4 to 4
- values: bfloat16 [8192, 4096], P('ctx', 'frame'), may hold values from -6 to 6
- query_frames: int32 [256], P('ctx'), may hold values from 0 to 383, as said below
- frame_counts: int32 [512], replicated, may hold values from 0 to 16, as said below
- clip_of_frame: int32 [256], P('ctx'), may hold values from 0 to 15, as said below
- in_proj: bfloat16 [4096, 1024], P('frame'), may hold values from -0.09375 to 0.09375
- mlp_up: bfloat16 [1024, 4096], replicated, may hold values from -0.1875 to 0.1875
- mlp_down: bfloat16 [4096, 1024], replicated, may hold values from -0.09375 to 0.09375
- reward_head: float32 [1024], replicated, may hold values from -0.1875 to 0.1875
Outputs:
- query_grad: float32 [4096, 4096], P('ctx', 'frame')
- key_grad: float32 [8192, 4096], P('ctx', 'frame')
- value_grad: float32 [8192, 4096], P('ctx', 'frame')
- clip_reward: float32 [128], P(('ctx', 'frame'))
Inputs may be any that keep to these rules, and one draw needn't show every extreme that they name: `query_frames`: the query patch rows are distinct rows of the first 512 * 3 // 4 patch rows of the video, in increasing order, all of them live; the first and the last of those rows are always among them. `frame_counts`: the live tokens are a prefix of the sequence of at least three quarters of it: rows before the prefix's end are full, one row may be partly live, the rows after it have none, and the last row has none. `clip_of_frame`: within each aligned block of 32 patch row slots every clip number appears exactly 2 times.
All inputs are finite; a program needn't handle non-finite values.
Results may differ from a plain program's by a relative error of at most 0.02.
Values may be sent and summed in bfloat16 or wider, within the bound.
No kernel may reach another device: no remote copies, remote signals or barrier semaphores. Data moves between devices by JAX's collectives and lax.ppermute only.
A program may use at most 192 MiB of HBM per device.

v0:
```python
import functools
import math

import jax
import jax.numpy as jnp
from jax import lax
from jax.experimental import pallas as pl
from jax.experimental.pallas import tpu as pltpu
from jax.sharding import PartitionSpec as P

HD = 128
FTOK = 16
CLIP = 2
EPSILON = 1e-05
SCALE = 1.0 / math.sqrt(HD)
EXP2_SCALE = SCALE * math.log2(math.e)
DEAD = -1e30
EXTRA = 16
CHUNK = 512


f32 = jnp.float32
bf16 = jnp.bfloat16

NN = (((1,), (0,)), ((), ()))
NT = (((1,), (1,)), ((), ()))
TN = (((0,), (0,)), ((), ()))

VMEM = pl.BlockSpec(memory_space=pltpu.VMEM)
SMEM = pl.BlockSpec(memory_space=pltpu.SMEM)


def dot(left, right, dims):
    return lax.dot_general(left, right, dims, preferred_element_type=f32)


def call(kernel, in_specs, outs, scratch=(), work=0, limit=8):
    return pl.pallas_call(
        kernel,
        cost_estimate=pl.CostEstimate(flops=work, transcendentals=0, bytes_accessed=1 << 20),
        out_shape=[jax.ShapeDtypeStruct(shape, dtype) for shape, dtype in outs],
        in_specs=in_specs,
        out_specs=[VMEM] * len(outs),
        scratch_shapes=list(scratch),
        compiler_params=pltpu.CompilerParams(vmem_limit_bytes=limit * 1024 * 1024),
    )


def split3(x):
    high = x.astype(bf16).astype(f32)
    rest = x - high
    middle = rest.astype(bf16).astype(f32)
    low = (rest - middle).astype(bf16).astype(f32)
    return high, middle, low


def angles(frame):
    lane = lax.broadcasted_iota(jnp.int32, (1, HD), 1).astype(f32)
    half_width = HD // 2
    lane = jnp.where(lane < half_width, lane, lane - half_width)
    angle = frame * jnp.exp(lane * (-math.log(10000.0) / half_width))
    return jnp.cos(angle), jnp.sin(angle)


def spread_angles(table):
    slots = table.shape[1] - FTOK
    cf, sf = table[0, :slots, :], table[1, :slots, :]
    ct, st = table[0, slots:, :], table[1, slots:, :]
    c = cf[:, None, :] * ct[None] - sf[:, None, :] * st[None]
    s = sf[:, None, :] * ct[None] + cf[:, None, :] * st[None]
    rows = slots * FTOK
    lane = lax.broadcasted_iota(jnp.int32, (rows, HD), 1)
    return c.reshape(rows, HD), jnp.where(lane < HD // 2, -1.0, 1.0) * s.reshape(rows, HD)


def fill_table(table, frames):
    slots = table.shape[1] - FTOK
    table[0, :slots, :], table[1, :slots, :] = angles(frames * FTOK)
    token = lax.broadcasted_iota(jnp.int32, (FTOK, HD), 0).astype(f32)
    table[0, slots:, :], table[1, slots:, :] = angles(token)


def rotate_kernel(ctx, frames_any, q_any, k_any, v_any, *refs):
    kv_own, kv_send, kv_high, key_table, q_own, q_send, query_table = refs[:7]
    q, k, v, frames, places, sems = refs[7:]
    pairs = ((k_any, k), (v_any, v), (q_any, q), (frames_any, frames))
    copies = [pltpu.make_async_copy(one, two, sems.at[i]) for i, (one, two) in enumerate(pairs)]
    for copy in copies:
        copy.start()
    slots = k.shape[0] // FTOK
    row = lax.broadcasted_iota(jnp.int32, (slots, HD), 0)
    fill_table(key_table, (row + ctx[0] * slots).astype(f32))
    c, s = spread_angles(key_table)
    for copy in copies:
        copy.wait()
    high = kv_high.shape[0]
    for which in range(2):

        @pl.when(ctx[0] % 2 == which)
        def _():
            for side, out in ((which, kv_own), (1 - which, kv_send)):
                cols = slice(side * HD, side * HD + HD)
                head = k[:, cols].astype(f32)
                turned = head * c + pltpu.roll(head, HD // 2, 1) * s
                out[:, :HD] = turned.astype(bf16)
                out[:, HD:] = v[:, cols]

    kv_high[...] = kv_send[-high:, :]
    for i in range(places.shape[0]):
        places[i : i + 1, :] = jnp.full((1, HD), frames[i].astype(f32))
    fill_table(query_table, places[...])
    c, s = spread_angles(query_table)
    for which in range(2):

        @pl.when(ctx[0] % 2 == which)
        def _():
            for side, out in ((which, q_own), (1 - which, q_send)):
                head = q[:, side * HD : side * HD + HD].astype(f32)
                turned = head * c + pltpu.roll(head, HD // 2, 1) * s
                out[...] = turned.T.astype(bf16)


def plan_kernel(frame, clips, frames, counts, place, live, seen):
    slots = clips.shape[0]
    for i in range(seen.shape[0]):
        seen[i] = 0
    lane = lax.broadcasted_iota(jnp.int32, place.shape, 1)
    slot = lane // FTOK
    total = jnp.zeros(place.shape, jnp.int32)
    for i in range(slots):
        clip = clips[i]
        rank = seen[clip]
        seen[clip] = rank + 1
        away = clip ^ frame[0]
        spot = (((away // 8) * 2 + away % 2) * 4 + (away // 2) % 4) * CLIP + rank
        total = jnp.where(slot == i, spot * FTOK, total)

        @pl.when(away == 0)
        def _():
            live[rank] = counts[frames[i]]

    place[...] = total + lane % FTOK


def fill_keys(ctx, counts, starts, kv_refs, kaug):
    rows = kv_refs[0].shape[0]
    lane = lax.broadcasted_iota(jnp.int32, (rows, HD), 1)
    row = lax.broadcasted_iota(jnp.int32, (rows, HD), 0)
    ones = jnp.where((lane >= 3) & (lane < 6), 1.0, 0.0)
    live = jnp.sum(jnp.sum(counts[...].astype(f32), axis=0, keepdims=True), axis=1, keepdims=True)
    me = ctx[0]
    owners = (me, me ^ 1, 6 - me + 2 * (me % 2), 7 - me)
    for part, ref in enumerate(kv_refs):
        owner, index, parts = starts[part]
        place = (row + (owners[owner] * parts + index) * rows).astype(f32)
        bias = jnp.where(place < live, 0.0, DEAD)
        kaug[part * rows : part * rows + rows, :HD] = ref[:, :HD]
        kaug[part * rows : part * rows + rows, HD:] = jnp.where(lane == 6, bias, ones).astype(bf16)


def forward_kernel(ctx, counts, *refs, blocks, starts, first, last):
    refs = list(refs)

    def take(count):
        taken = refs[:count]
        del refs[:count]
        return taken

    pieces = len(starts)
    if first:
        q_refs = take(blocks)
    else:
        (q_all,) = take(1)
    kv_refs = take(pieces)
    if not first:
        acc_in, stat_in = take(2)
    if last:
        out_refs = take(blocks)
    else:
        acc_out, stat_out = take(2)
    if first:
        (q_all,) = take(1)
    kaug, v_t, *scores = take(4)
    if last:
        (out_all,) = take(1)
    rows = kv_refs[0].shape[0]
    keys = pieces * rows
    wide = q_all.shape[2]
    fill_keys(ctx, counts, starts, kv_refs, kaug)
    for part, ref in enumerate(kv_refs):
        v_t[:, part * rows : part * rows + rows] = ref[:, HD:].astype(f32).T.astype(bf16)
    if first:
        sub = lax.broadcasted_iota(jnp.int32, (HD, wide), 0)
        tail = jnp.where(sub == 6, 1.0, 0.0).astype(bf16)
        for i in range(blocks):
            q_all[i, :HD, :] = q_refs[i][...]
            q_all[i, HD:, :] = tail
    spans = [slice(j * CHUNK, j * CHUNK + CHUNK) for j in range(keys // CHUNK)]

    def score(i, slot, span, top):
        s = dot(kaug[span, :], q_all[i], NN)
        scores[slot][span, :] = s
        return jnp.maximum(top, jnp.max(s, axis=0, keepdims=True))

    def start(i):
        return jnp.full((1, wide), -jnp.inf, f32) if first else stat_in[i, 0:1, :]

    def block(i, slot, top, follow):
        if first:
            total = jnp.zeros((1, wide), f32)
            acc = jnp.zeros((HD, wide), f32)
        else:
            shrink = jnp.exp2((stat_in[i, 0:1, :] - top) * EXP2_SCALE)
            total = stat_in[i, 1:2, :] * shrink
            acc = acc_in[i] * shrink
        following = start(follow)
        for span in spans:
            following = score(follow, 1 - slot, span, following)
            p = jnp.exp2((scores[slot][span, :] - top) * EXP2_SCALE)
            total = total + jnp.sum(p, axis=0, keepdims=True)
            acc = acc + dot(v_t[:, span], p.astype(bf16), NN)
        if not last:
            acc_out[i] = acc
            which = lax.broadcasted_iota(jnp.int32, (8, wide), 0)
            stat_out[i] = jnp.where(which == 0, top, total)
        else:
            out_all[i, :HD, :] = (acc / total).astype(bf16)
            high, middle, low = split3(top + jnp.log(total) * (1.0 / SCALE))
            which = lax.broadcasted_iota(jnp.int32, (EXTRA, wide), 0)
            rest = jnp.where(which == 1, middle, jnp.where(which == 2, low, 0.0))
            out_all[i, HD:, :] = jnp.where(which == 0, high, rest).astype(bf16)
        return following

    top = start(0)
    for span in spans:
        top = score(0, 0, span, top)

    def pair(t, top):
        middle = block(2 * t, 0, top, 2 * t + 1)
        return block(2 * t + 1, 1, middle, jnp.minimum(2 * t + 2, blocks - 1))

    lax.fori_loop(0, blocks // 2, pair, top)
    if last:
        for i in range(blocks):
            out_refs[i][...] = out_all[i]


def forward(ctx, counts, q_blocks, kv_pieces, starts, before=(), last=False):
    first = not before
    blocks, wide = (len(q_blocks), q_blocks[0].shape[1]) if first else q_blocks.shape[::2]
    keys = len(kv_pieces) * kv_pieces[0].shape[0]
    if last:
        outs = [((HD + EXTRA, wide), bf16)] * blocks
    else:
        outs = [((blocks, HD, wide), f32), ((blocks, 8, wide), f32)]
    if first:
        outs.append(((blocks, 2 * HD, wide), bf16))
    args = [*(q_blocks if first else [q_blocks]), *kv_pieces, *before]
    return call(
        functools.partial(forward_kernel, blocks=blocks, starts=starts, first=first, last=last),
        [SMEM] + [VMEM] * (len(args) + 1),
        outs,
        [
            pltpu.VMEM((keys, 2 * HD), bf16),
            pltpu.VMEM((HD, keys), bf16),
            pltpu.VMEM((keys, wide), f32),
            pltpu.VMEM((keys, wide), f32),
        ]
        + ([pltpu.VMEM((blocks, HD + EXTRA, wide), bf16)] if last else []),
        work=10**10,
        limit=13 if first else 8,
    )(ctx, counts, *args)


def one_hot(place):
    rows = place.shape[1]
    row = lax.broadcasted_iota(jnp.int32, (rows, rows), 0)
    return jnp.where(row == place[...], 1.0, 0.0).astype(bf16)


def combine_kernel(ctx, place, *refs):
    partial, (out_t, logs, c0, c1, c2, c3) = refs[:4], refs[4:]
    wide = partial[0].shape[1]
    for side in range(2):
        sums = []
        for ref in partial[2 * side : 2 * side + 2]:
            tail = ref[HD:, :].astype(f32)
            sums.append(tail[0:1] + tail[1:2] + tail[2:3])
        top = functools.reduce(jnp.maximum, sums)
        weight = [jnp.exp2((s - top) * EXP2_SCALE) for s in sums]
        total = sum(weight)
        acc = jnp.zeros((HD, wide), f32)
        for w, ref in zip(weight, partial[2 * side : 2 * side + 2]):
            acc = acc + (w / total) * ref[:HD, :].astype(f32)
        logs[side, :, :] = jnp.broadcast_to(top + jnp.log(total) * (1.0 / SCALE), (8, wide))
        head = ctx[0] % 2 if side == 0 else 1 - ctx[0] % 2
        out_t[pl.ds(pl.multiple_of(head * HD, HD), HD), :] = acc.astype(bf16)
    grouped = dot(one_hot(place), out_t[...], NT).astype(bf16)
    quarter = wide // 4
    for i, ref in enumerate((c0, c1, c2, c3)):
        ref[...] = grouped[i * quarter : i * quarter + quarter]


def project_kernel(o0, o1, o2, o3, w0, w1, w2, w3, x0, x1, x2, x3):
    total = None
    for o, w in ((o0, w0), (o1, w1), (o2, w2), (o3, w3)):
        term = dot(o[...], w[...], NN)
        total = term if total is None else total + term
    rows = x0.shape[0]
    for i, ref in enumerate((x0, x1, x2, x3)):
        ref[...] = total[i * rows : i * rows + rows].astype(ref.dtype)


def unproject_kernel(g0, g1, g2, g3, w0, w1, w2, w3, d0, d1, d2, d3, g):
    rows = g0.shape[0]
    for i, ref in enumerate((g0, g1, g2, g3)):
        g[i * rows : i * rows + rows, :] = ref[...]
    for w, d in ((w0, d0), (w1, d1), (w2, d2), (w3, d3)):
        d[...] = dot(g[...], w[...], NT).astype(bf16)


def center(x):
    mean = jnp.mean(x, axis=1, keepdims=True)
    shifted = x - mean
    rate = lax.rsqrt(jnp.mean(shifted * shifted, axis=1, keepdims=True) + EPSILON)
    return shifted * rate, rate


def center_grad(grad, normed, rate):
    return rate * (
        grad
        - jnp.mean(grad, axis=1, keepdims=True)
        - normed * jnp.mean(grad * normed, axis=1, keepdims=True)
    )


def reward_kernel(counts, x0, x1, x2, x3, head, up, down, grad_out, reward_out, slopes):
    steps, _, part = slopes.shape
    vision = up.shape[0]

    def piece(j):
        return pl.ds(pl.multiple_of(j * part, part), part)

    rows = x0.shape[0]

    def live(shape, axis):
        row = lax.broadcasted_iota(jnp.int32, shape, axis)
        left = jnp.where(row < FTOK, counts[0], counts[1] + FTOK)
        return jnp.where(row < left, 1.0, 0.0)

    x = x0[...].astype(f32) + x1[...].astype(f32) + x2[...].astype(f32) + x3[...].astype(f32)
    normed, rate = center(x)
    low_normed = normed.astype(bf16)
    c0 = math.sqrt(2.0 / math.pi)
    c1 = 0.044715

    def upward(j, hidden):
        before = dot(low_normed, up[:, piece(j)], NN)
        square = before * before
        tanh = jnp.tanh(c0 * before * (1.0 + c1 * square))
        half = 0.5 * (1.0 + tanh)
        slope = half + 0.5 * before * (1.0 - tanh * tanh) * (c0 * (1.0 + 3.0 * c1 * square))
        slopes[j] = slope
        return hidden + dot((before * half).astype(bf16), down[piece(j), :], NN)

    hidden = lax.fori_loop(0, steps, upward, jnp.zeros((rows, vision), f32))
    alive = live((rows, 1), 0)
    count = jnp.sum(alive, axis=0, keepdims=True)
    pooled = jnp.sum(hidden * alive, axis=0, keepdims=True) / count
    pooled_normed, pooled_rate = center(pooled)
    reward = count * jnp.sum(pooled_normed * head[...], axis=1, keepdims=True)
    reward_out[...] = jnp.broadcast_to(reward, reward_out.shape)
    pooled_grad = center_grad(count * head[...], pooled_normed, pooled_rate) / count
    high, middle, low = split3(pooled_grad)
    which = lax.broadcasted_iota(jnp.int32, (EXTRA, vision), 0)
    pieces = jnp.where(which == 0, high, jnp.where(which == 1, middle, jnp.where(which == 2, low, 0.0)))
    pieces_b = pieces.astype(bf16)
    alive_t = live((1, rows), 1)

    def downward(j, normed_grad):
        spread = jnp.sum(dot(pieces_b, down[piece(j), :], NT), axis=0, keepdims=True)
        before_grad = (spread * slopes[j] * alive).astype(bf16)
        return normed_grad + dot(before_grad, up[:, piece(j)], NT)

    normed_grad = lax.fori_loop(0, steps, downward, jnp.zeros((rows, vision), f32))
    grad_out[...] = center_grad(normed_grad, normed, rate).astype(bf16)


def reward_call(counts, inputs, head, mlp_up, mlp_down):
    vision, hidden = mlp_up.shape
    steps = 8
    part = hidden // steps
    rows = inputs[0].shape[0]
    return call(
        reward_kernel,
        [SMEM] + [VMEM] * 7,
        [((rows, vision), bf16), ((8, HD), f32)],
        [
            pltpu.VMEM((steps, rows, part), f32),
        ],
    )(counts, *inputs, head.reshape(1, -1), mlp_up, mlp_down)


def ungroup_kernel(ctx, place, d0, d1, d2, d3, out_t, logs, ps, po, grad):
    quarter = d0.shape[0]
    for i, ref in enumerate((d0, d1, d2, d3)):
        grad[i * quarter : i * quarter + quarter, :] = ref[...]
    wide = place.shape[1]
    grad_t = dot(grad[...], one_hot(place), TN)
    product = grad_t * out_t[...].astype(f32)
    which = lax.broadcasted_iota(jnp.int32, (EXTRA, wide), 0)
    for head in range(2):
        delta = jnp.sum(product[head * HD : head * HD + HD], axis=0, keepdims=True)
        for side, ref in enumerate((ps, po)):

            @pl.when(head == (ctx[0] % 2 if side == 0 else 1 - ctx[0] % 2))
            def _():
                ref[:HD, :] = grad_t[head * HD : head * HD + HD].astype(bf16)
                rows = split3(delta) + split3(-logs[side, 0:1, :])
                tail = jnp.where(which == 6, 1.0, 0.0)
                for i, piece in enumerate(rows):
                    tail = jnp.where(which == i, piece, tail)
                ref[HD:, :] = tail.astype(bf16)


def backward_kernel(ctx, counts, *refs, blocks, starts, first, last):
    refs = list(refs)

    def take(count):
        taken = refs[:count]
        del refs[:count]
        return taken

    pieces = len(starts)
    (q_in,) = take(1)
    g_refs = take(blocks)
    kv_refs = take(pieces)
    if not first:
        (dq_in,) = take(1)
    dq_refs = take(blocks) if last else take(1)
    out_refs = take(2) if last else take(1)
    kaug, vaug, k_t, q_all, g_all, dk, dv = take(7)
    if last:
        (dq_all,) = take(1)
    rows = kv_refs[0].shape[0]
    keys = pieces * rows
    wide = q_in.shape[2]
    fill_keys(ctx, counts, starts, kv_refs, kaug)
    lane = lax.broadcasted_iota(jnp.int32, (rows, HD), 1)
    minus = jnp.where(lane < 3, -1.0, 0.0).astype(bf16)
    for part, ref in enumerate(kv_refs):
        where = slice(part * rows, part * rows + rows)
        vaug[where, :HD] = ref[:, HD:]
        vaug[where, HD:] = minus
        k_t[:, where] = ref[:, :HD].astype(f32).T.astype(bf16)
    dk[...] = jnp.zeros_like(dk)
    dv[...] = jnp.zeros_like(dv)
    blank = jnp.zeros((HD - EXTRA, wide), bf16)
    for i in range(blocks):
        q_all[i, :HD, :] = q_in[i, :HD, :]
        q_all[i, HD : HD + EXTRA, :] = g_refs[i][HD:, :]
        q_all[i, HD + EXTRA :, :] = blank
        g_all[i, : HD + EXTRA, :] = g_refs[i][...]
        g_all[i, HD + EXTRA :, :] = blank

    def block(i, carry):
        query = q_all[i]
        grad = g_all[i]
        acc = jnp.zeros((HD, wide), f32) if first else dq_in[i]
        for j in range(keys // CHUNK):
            part = slice(j * CHUNK, j * CHUNK + CHUNK)
            p = jnp.exp2(dot(kaug[part, :], query, NN) * EXP2_SCALE)
            ds = (p * dot(vaug[part, :], grad, NN)).astype(bf16)
            dv[part, :] += dot(p.astype(bf16), grad[:HD], NT)
            dk[part, :] += dot(ds, query[:HD], NT)
            acc = acc + dot(k_t[:, part], ds, NN)
        if last:
            dq_all[i] = (acc * SCALE).astype(bf16)
        else:
            dq_refs[0][i] = acc
        return carry

    lax.fori_loop(0, blocks, block, 0)
    if last:
        for i in range(blocks):
            dq_refs[i][...] = dq_all[i]
    if last:
        out_refs[0][...] = dk[...] * SCALE
        out_refs[1][...] = dv[...]
    else:
        out_refs[0][:, :HD] = (dk[...] * SCALE).astype(bf16)
        out_refs[0][:, HD:] = dv[...].astype(bf16)


def backward(ctx, counts, q_blocks, g_blocks, kv_pieces, starts, before=None, last=False):
    blocks, _, wide = q_blocks.shape
    pieces = len(kv_pieces)
    rows = kv_pieces[0].shape[0]
    keys = pieces * rows
    if last:
        outs = [((HD, wide), bf16)] * blocks + [((keys, HD), f32)] * 2
    else:
        outs = [((blocks, HD, wide), f32), ((keys, 2 * HD), bf16)]
    scratch = [
        pltpu.VMEM((keys, 2 * HD), bf16),
        pltpu.VMEM((keys, 2 * HD), bf16),
        pltpu.VMEM((HD, keys), bf16),
        pltpu.VMEM((blocks, 2 * HD, wide), bf16),
        pltpu.VMEM((blocks, 2 * HD, wide), bf16),
        pltpu.VMEM((keys, HD), f32),
        pltpu.VMEM((keys, HD), f32),
    ]
    if last:
        scratch.append(pltpu.VMEM((blocks, HD, wide), bf16))
    args = [q_blocks, *g_blocks, *kv_pieces] + ([] if before is None else [before])
    out = call(
        functools.partial(
            backward_kernel, blocks=blocks, starts=starts, first=before is None, last=last
        ),
        [SMEM] + [VMEM] * (len(args) + 1),
        outs,
        scratch,
        work=2 * 10**10,
    )(ctx, counts, *args)
    count = blocks if last else 1
    return (out[:blocks] if last else out[0]), out[count:]


def unrotate(x, c, s):
    return x * c - pltpu.roll(x, HD // 2, 1) * s


def query_grad_kernel(ctx, table, d0, d1, d2, d3, out):
    c, s = spread_angles(table)
    for which in range(2):

        @pl.when(ctx[0] % 2 == which)
        def _():
            for head, one, two in ((which, d0, d1), (1 - which, d2, d3)):
                total = one[...].astype(f32) + two[...].astype(f32)
                out[:, head * HD : head * HD + HD] = unrotate(total.T, c, s)


def key_grad_kernel(ctx, table, dk, dv, far, par, far_par, dk_out, dv_out):
    c, s = spread_angles(table)
    for which in range(2):

        @pl.when(ctx[0] % 2 == which)
        def _():
            cols = slice(which * HD, which * HD + HD)
            dk_out[:, cols] = unrotate(dk[...] + far[:, :HD].astype(f32), c, s)
            dv_out[:, cols] = dv[...] + far[:, HD:].astype(f32)
            cols = slice(HD - which * HD, 2 * HD - which * HD)
            total = par[...].astype(f32) + far_par[...].astype(f32)
            dk_out[:, cols] = unrotate(total[:, :HD], c, s)
            dv_out[:, cols] = total[:, HD:]


def ctx_swap(turn, flip):
    def target(x, z):
        x = (x, x ^ 1, 3 - x)[turn]
        return x * 2 + (z ^ flip)

    return [(x * 2 + z, target(x, z)) for x in range(4) for z in range(2)]


def send_ctx(array, turn, flip):
    return lax.ppermute(array, "ctx", ctx_swap(turn, flip))


def frame_xor(mask):
    return [(i, i ^ mask) for i in range(16)]


QUAD_MASKS = (0, 1, 8, 9)
Y_MASKS = (0, 2, 4, 6)


def send_frame(array, mask):
    return array if mask == 0 else lax.ppermute(array, "frame", frame_xor(mask))


def exchange(blocks):
    same, near, other, near_other = blocks
    return [same, send_ctx(near, 1, 0), send_ctx(other, 0, 1), send_ctx(near_other, 1, 1)]


def shards(
    queries,
    keys,
    values,
    query_frames,
    frame_counts,
    clip_of_frame,
    in_proj,
    mlp_up,
    mlp_down,
    reward_head,
):
    ctx_index = lax.axis_index("ctx")
    frame_index = lax.axis_index("frame")
    query_rows = queries.shape[0]
    key_rows = keys.shape[0]
    frame_slots = query_frames.shape[0]
    ctx = ctx_index.reshape(1).astype(jnp.int32)
    counts = frame_counts.reshape(-1, HD)
    packed_rows = ((key_rows, 2 * HD), bf16)
    any_space = pl.BlockSpec(memory_space=pltpu.HBM)
    high_rows = key_rows // 2
    kv_own, kv_send, kv_high, key_table, qs, qo, query_table = call(
        rotate_kernel,
        [SMEM] + [any_space] * 4,
        [packed_rows] * 2
        + [((high_rows, 2 * HD), bf16), ((2, key_rows // FTOK + FTOK, HD), f32)]
        + [((HD, query_rows), bf16)] * 2
        + [((2, frame_slots + FTOK, HD), f32)],
        [
            pltpu.VMEM(queries.shape, bf16),
            pltpu.VMEM(keys.shape, bf16),
            pltpu.VMEM(values.shape, bf16),
            pltpu.SMEM((frame_slots,), jnp.int32),
            pltpu.VMEM((frame_slots, HD), f32),
            pltpu.SemaphoreType.DMA((4,)),
        ],
    )(ctx, query_frames, queries, keys, values)
    kv_far = send_ctx(kv_own, 2, 0)
    q_blocks = exchange((qs, qs, qo, qo))
    kv_par = send_ctx(kv_send, 0, 1)

    place, my_counts = pl.pallas_call(
        plan_kernel,
        out_shape=[
            jax.ShapeDtypeStruct((1, query_rows), jnp.int32),
            jax.ShapeDtypeStruct((CLIP,), jnp.int32),
        ],
        in_specs=[SMEM] * 4,
        out_specs=[VMEM, SMEM],
        scratch_shapes=[pltpu.SMEM((frame_slots // CLIP,), jnp.int32)],
        compiler_params=pltpu.CompilerParams(vmem_limit_bytes=8 * 1024 * 1024),
    )(frame_index.reshape(1).astype(jnp.int32), clip_of_frame, query_frames, frame_counts)

    *state, q_blocks = forward(
        ctx, counts, q_blocks, (kv_own, kv_far), ((0, 0, 1), (2, 0, 1))
    )
    kv_high, _ = lax.optimization_barrier((kv_high, state[1]))
    kv_par, _ = lax.optimization_barrier((kv_par, state[1]))
    kv_far_high = send_ctx(kv_high, 2, 1)
    kv_far_low = send_ctx(kv_par[:high_rows], 2, 0)
    state = forward(ctx, counts, q_blocks, (kv_par,), ((1, 0, 1),), state)
    in_proj, _ = lax.optimization_barrier((in_proj, state[1]))
    near = send_frame(in_proj, 8)
    kv_far_par = (kv_far_low, kv_far_high)
    far_par = ((3, 0, 2), (3, 1, 2))
    partial = forward(ctx, counts, q_blocks, kv_far_par, far_par, state, True)
    in_proj, near_late, _ = lax.optimization_barrier((in_proj, near, partial[0]))
    weights = (in_proj, send_frame(in_proj, 1), near_late, send_frame(near_late, 1))
    partial = exchange(partial)
    width = queries.shape[1]
    quarter = query_rows // 4
    out_t, logs, *chunks = call(
        combine_kernel,
        [SMEM] + [VMEM] * 5,
        [((width, query_rows), bf16), ((2, 8, query_rows), f32)] + [((quarter, width), bf16)] * 4,
        work=5 * 10**9,
    )(ctx, place, *partial)
    chunks = [send_frame(chunk, mask) for chunk, mask in zip(chunks, QUAD_MASKS)]
    vision = in_proj.shape[1]
    clip_rows = CLIP * FTOK
    inputs = call(
        project_kernel,
        [VMEM] * 8,
        [((clip_rows, vision), f32)] + [((clip_rows, vision), bf16)] * 3,
        work=5 * 10**9,
    )(*chunks, *weights)
    inputs = [send_frame(x, mask) for x, mask in zip(inputs, Y_MASKS)]
    input_grad, reward = reward_call(my_counts, inputs, reward_head, mlp_up, mlp_down)
    grads = [send_frame(input_grad, mask) for mask in Y_MASKS]
    grads = call(
        unproject_kernel,
        [VMEM] * 8,
        [((quarter, width), bf16)] * 4,
        [pltpu.VMEM((quarter, vision), bf16)],
    )(*grads, *weights)
    grads = [send_frame(grad, mask) for grad, mask in zip(grads, QUAD_MASKS)]
    packed = (HD + EXTRA, query_rows)
    gs, go = call(
        ungroup_kernel,
        [SMEM] + [VMEM] * 7,
        [(packed, bf16)] * 2,
        [pltpu.VMEM((query_rows, width), bf16)],
    )(ctx, place, *grads, out_t, logs)
    g_blocks = exchange((gs, gs, go, go))
    dq, (d_far_par,) = backward(ctx, counts, q_blocks, g_blocks, kv_far_par, far_par)
    d_far_par = send_ctx(d_far_par, 2, 1)
    dq, (d_par,) = backward(ctx, counts, q_blocks, g_blocks, (kv_par,), ((1, 0, 1),), dq)
    d_par = send_ctx(d_par, 0, 1)
    dq, (d_far,) = backward(ctx, counts, q_blocks, g_blocks, (kv_far,), ((2, 0, 1),), dq)
    d_far = send_ctx(d_far, 2, 0)
    dq, (dk_own, dv_own) = backward(
        ctx, counts, q_blocks, g_blocks, (kv_own,), ((0, 0, 1),), dq, True
    )
    dq = exchange(dq)
    (query_grad,) = call(
        query_grad_kernel,
        [SMEM] + [VMEM] * 5,
        [((query_rows, width), f32)],
    )(ctx, query_table, *dq)
    key_grad, value_grad = call(
        key_grad_kernel,
        [SMEM] + [VMEM] * 6,
        [((key_rows, width), f32)] * 2,
    )(ctx, key_table, dk_own, dv_own, d_far, d_par, d_far_par)
    return query_grad, key_grad, value_grad, reward[0, :1]


def solution(mesh):
    return jax.shard_map(
        shards,
        mesh=mesh,
        in_specs=(
            P("ctx", "frame"),
            P("ctx", "frame"),
            P("ctx", "frame"),
            P("ctx"),
            P(),
            P("ctx"),
            P("frame", None),
            P(),
            P(),
            P(),
        ),
        out_specs=(P("ctx", "frame"), P("ctx", "frame"), P("ctx", "frame"), P(("ctx", "frame"))),
        check_vma=False,
    )
```

profile of v0, /device:TPU:0, one launch (start us, length us, event | category | flops | bytes accessed | tf_op | source)
XLA Modules:
  0.0 176.7 jit_solution(11959703657277895648)
XLA Ops:
  5.8 2.9 %collective-permute-start.3 = (bf16[1024,256]{1,0:T(8,128)(2,1)S(1)}, bf16[1024,256]{1,0:T(8,128)(2,1)S(1)}, u32[]{:S(2)}, u32[]{:S(2)}) collective-permute-start(bf16[1024,256]{1,0:T(8,128)(2,1)S(1)} %get-tuple-element.62.refs_4_.refs_5_), channel_id=1, source_target_pairs={{0,96},{16,112},{32,64},{48,80},{64,32},{80,48},{96,0},{112,16},{1... | collective-permute-start | bytes 1572872 | tf_op jit(solution)/shard_map/ppermute | solution.py:568
  9.0 5.1 %collective-permute-start.2 = (bf16[128,512]{1,0:T(8,128)(2,1)S(1)}, bf16[128,512]{1,0:T(8,128)(2,1)S(1)}, u32[]{:S(2)}, u32[]{:S(2)}) collective-permute-start(bf16[128,512]{1,0:T(8,128)(2,1)S(1)} %get-tuple-element.61), channel_id=1, source_target_pairs={{0,48},{16,32},{32,16},{48,0},{64,112},{80,96},{96,80},{112,64},{1... | collective-permute-start | bytes 393224 | tf_op jit(solution)/shard_map/ppermute | solution.py:568
  14.1 3.5 %collective-permute-start.4 = (bf16[1024,256]{1,0:T(8,128)(2,1)S(1)}, bf16[1024,256]{1,0:T(8,128)(2,1)S(1)}, u32[]{:S(2)}, u32[]{:S(2)}) collective-permute-start(bf16[1024,256]{1,0:T(8,128)(2,1)S(1)} %get-tuple-element.66), channel_id=1, source_target_pairs={{0,16},{16,0},{32,48},{48,32},{64,80},{80,64},{96,112},{112,96},{1... | collective-permute-start | bytes 1572872 | tf_op jit(solution)/shard_map/ppermute | solution.py:568
  19.9 2.8 %collective-permute-done.1.refs_2_ = bf16[128,512]{1,0:T(8,128)(2,1)S(1)} collective-permute-done((bf16[128,512]{1,0:T(8,128)(2,1)S(1)}, bf16[128,512]{1,0:T(8,128)(2,1)S(1)}, u32[]{:S(2)}, u32[]{:S(2)}) %collective-permute-start.1) | collective-permute-done | bytes 131104 | tf_op jit(solution)/shard_map/ppermute | solution.py:568
  23.4 6.0 %shard_map.130 = (f32[4,128,512]{2,1,0:T(8,128)S(1)}, f32[4,8,512]{2,1,0:T(8,128)S(1)}, bf16[4,256,512]{2,1,0:T(8,128)(2,1)S(1)}) custom-call(s32[1]{0:T(128)} %bitcast.ctx, s32[4,128]{1,0:T(4,128)S(1)} %bitcast.10, bf16[128,512]{1,0:T(8,128)(2,1)S(1)} %get-tuple-element.60.refs_0_, bf16[128,512]{1,0:T(8,128)(2,1)S(1)} %collective-permute-done.refs_1_, ...), custom_call_target="tpu_custom_call" | custom-call | flops 10000000000 | bytes 1048576 | tf_op jit(solution)/shard_map/pallas_call | solution.py:259
  29.5 3.8 %collective-permute-done.4.refs_1_.refs_5_ = bf16[1024,256]{1,0:T(8,128)(2,1)S(1)} collective-permute-done((bf16[1024,256]{1,0:T(8,128)(2,1)S(1)}, bf16[1024,256]{1,0:T(8,128)(2,1)S(1)}, u32[]{:S(2)}, u32[]{:S(2)}) %collective-permute-start.4) | collective-permute-done | bytes 524320 | tf_op jit(solution)/shard_map/ppermute | solution.py:568
  33.8 3.0 %collective-permute-start.6 = (bf16[512,256]{1,0:T(8,128)(2,1)S(1)}, bf16[512,256]{1,0:T(8,128)(2,1)S(1)}, u32[]{:S(2)}, u32[]{:S(2)}) collective-permute-start(bf16[512,256]{1,0:T(8,128)(2,1)S(1)} %get-tuple-element.70), channel_id=1, source_target_pairs={{0,112},{16,96},{32,80},{48,64},{64,48},{80,32},{96,16},{112,0},{1... | collective-permute-start | bytes 786440 | tf_op jit(solution)/shard_map/ppermute | solution.py:568
  36.8 3.5 %shard_map.132 = (f32[4,128,512]{2,1,0:T(8,128)S(1)}, f32[4,8,512]{2,1,0:T(8,128)S(1)}) custom-call(s32[1]{0:T(128)} %bitcast.ctx, s32[4,128]{1,0:T(4,128)S(1)} %bitcast.11, bf16[4,256,512]{2,1,0:T(8,128)(2,1)S(1)} %get-tuple-element.63.refs_0_, bf16[1024,256]{1,0:T(8,128)(2,1)S(1)} %collective-permute-done.4.refs_1_.refs_5_, ...), custom_call_target="tpu_custom_call" | custom-call | flops 10000000000 | bytes 1048576 | tf_op jit(solution)/shard_map/pallas_call | solution.py:259
  43.8 4.9 %collective-permute-done.6.refs_2_.refs_6_ = bf16[512,256]{1,0:T(8,128)(2,1)S(1)} collective-permute-done((bf16[512,256]{1,0:T(8,128)(2,1)S(1)}, bf16[512,256]{1,0:T(8,128)(2,1)S(1)}, u32[]{:S(2)}, u32[]{:S(2)}) %collective-permute-start.6) | collective-permute-done | bytes 262176 | tf_op jit(solution)/shard_map/ppermute | solution.py:568
  48.6 4.3 %shard_map.133 = (bf16[144,512]{1,0:T(8,128)(2,1)S(1)}, bf16[144,512]{1,0:T(8,128)(2,1)}, bf16[144,512]{1,0:T(8,128)(2,1)}, bf16[144,512]{1,0:T(8,128)(2,1)}) custom-call(s32[1]{0:T(128)} %bitcast.ctx, s32[4,128]{1,0:T(4,128)S(1)} %bitcast.12, bf16[4,256,512]{2,1,0:T(8,128)(2,1)S(1)} %get-tuple-element.63.refs_0_, ...), custom_call_target="tpu_custom_call" | custom-call | flops 10000000000 | bytes 1048576 | tf_op jit(solution)/shard_map/pallas_call | solution.py:259
  60.9 5.3 %collective-permute-done.8.refs_2_ = bf16[144,512]{1,0:T(8,128)(2,1)} collective-permute-done((bf16[144,512]{1,0:T(8,128)(2,1)}, bf16[144,512]{1,0:T(8,128)(2,1)}, u32[]{:S(2)}, u32[]{:S(2)}) %collective-permute-start.8) | collective-permute-done | bytes 147488 | tf_op jit(solution)/shard_map/ppermute | solution.py:568
  70.6 3.2 %collective-permute-done.11.o2 = bf16[128,256]{1,0:T(8,128)(2,1)S(1)} collective-permute-done((bf16[128,256]{1,0:T(8,128)(2,1)S(1)}, bf16[128,256]{1,0:T(8,128)(2,1)S(1)}, u32[]{:S(2)}, u32[]{:S(2)}) %collective-permute-start.11) | collective-permute-done | bytes 65568 | tf_op jit(solution)/shard_map/ppermute | solution.py:580
  76.2 2.9 %collective-permute-start.17 = (bf16[32,1024]{1,0:T(8,128)(2,1)S(1)}, bf16[32,1024]{1,0:T(8,128)(2,1)S(1)}, u32[]{:S(2)}, u32[]{:S(2)}) collective-permute-start(bf16[32,1024]{1,0:T(8,128)(2,1)S(1)} %get-tuple-element.87), channel_id=1, source_target_pairs={{0,4},{1,5},{2,6},{3,7},{4,0},{5,1},{6,2},{7,3},{8,12},{9,13},{10,... | collective-permute-start | bytes 196616 | tf_op jit(solution)/shard_map/ppermute | solution.py:580
  79.4 3.6 %collective-permute-done.17.x2 = bf16[32,1024]{1,0:T(8,128)(2,1)S(1)} collective-permute-done((bf16[32,1024]{1,0:T(8,128)(2,1)S(1)}, bf16[32,1024]{1,0:T(8,128)(2,1)S(1)}, u32[]{:S(2)}, u32[]{:S(2)}) %collective-permute-start.17) | collective-permute-done | bytes 65568 | tf_op jit(solution)/shard_map/ppermute | solution.py:580
  84.7 11.8 %shard_map.136 = (bf16[32,1024]{1,0:T(8,128)(2,1)S(1)}, f32[8,128]{1,0:T(8,128)S(1)}) custom-call(s32[2]{0:T(128)S(1)} %get-tuple-element.65.counts, f32[32,1024]{1,0:T(8,128)S(1)} %get-tuple-element.85.x0, bf16[32,1024]{1,0:T(8,128)(2,1)S(1)} %collective-permute-done.16.x1, bf16[32,1024]{1,0:T(8,128)(2,1)S(1)} %collective-permute-done.17.x2, ...), custom_call_target="tpu_custom_call" | custom-call | bytes 1048576 | tf_op jit(solution)/shard_map/pallas_call | solution.py:394
  106.4 3.1 %collective-permute-done.23.d2 = bf16[128,256]{1,0:T(8,128)(2,1)S(1)} collective-permute-done((bf16[128,256]{1,0:T(8,128)(2,1)S(1)}, bf16[128,256]{1,0:T(8,128)(2,1)S(1)}, u32[]{:S(2)}, u32[]{:S(2)}) %collective-permute-start.23) | collective-permute-done | bytes 65568 | tf_op jit(solution)/shard_map/ppermute | solution.py:580
  115.5 4.2 %collective-permute-done.27.refs_4_ = bf16[144,512]{1,0:T(8,128)(2,1)S(1)} collective-permute-done((bf16[144,512]{1,0:T(8,128)(2,1)S(1)}, bf16[144,512]{1,0:T(8,128)(2,1)S(1)}, u32[]{:S(2)}, u32[]{:S(2)}) %collective-permute-start.27) | collective-permute-done | bytes 147488 | tf_op jit(solution)/shard_map/ppermute | solution.py:568
  122.1 6.2 %shard_map.139 = (f32[4,128,512]{2,1,0:T(8,128)S(1)}, bf16[1024,256]{1,0:T(8,128)(2,1)S(1)}) custom-call(s32[1]{0:T(128)} %bitcast.ctx, s32[4,128]{1,0:T(4,128)S(1)} %bitcast.13, bf16[4,256,512]{2,1,0:T(8,128)(2,1)S(1)} %copy-done.11, bf16[144,512]{1,0:T(8,128)(2,1)S(1)} %get-tuple-element.96.refs_1_, bf16[144,512]{1,0:T(8,128)(2,1)S(1)} %collective-permute-done.25.refs_2_, ...), custom_call_target="tpu_custom_call" | custom-call | flops 20000000000 | bytes 1048576 | tf_op jit(solution)/shard_map/pallas_call | solution.py:516
  128.3 6.2 %shard_map.140 = (f32[4,128,512]{2,1,0:T(8,128)S(1)}, bf16[1024,256]{1,0:T(8,128)(2,1)S(1)}) custom-call(s32[1]{0:T(128)} %bitcast.ctx, s32[4,128]{1,0:T(4,128)S(1)} %bitcast.14, bf16[4,256,512]{2,1,0:T(8,128)(2,1)S(1)} %copy-done.11, bf16[144,512]{1,0:T(8,128)(2,1)S(1)} %get-tuple-element.96.refs_1_, bf16[144,512]{1,0:T(8,128)(2,1)S(1)} %collective-permute-done.25.refs_2_, ...), custom_call_target="tpu_custom_call" | custom-call | flops 20000000000 | bytes 1048576 | tf_op jit(solution)/shard_map/pallas_call | solution.py:516
  134.6 6.2 %shard_map.141 = (f32[4,128,512]{2,1,0:T(8,128)S(1)}, bf16[1024,256]{1,0:T(8,128)(2,1)S(1)}) custom-call(s32[1]{0:T(128)} %bitcast.ctx, s32[4,128]{1,0:T(4,128)S(1)} %bitcast.15, bf16[4,256,512]{2,1,0:T(8,128)(2,1)S(1)} %copy-done.11, bf16[144,512]{1,0:T(8,128)(2,1)S(1)} %get-tuple-element.96.refs_1_, bf16[144,512]{1,0:T(8,128)(2,1)S(1)} %collective-permute-done.25.refs_2_, ...), custom_call_target="tpu_custom_call" | custom-call | flops 20000000000 | bytes 1048576 | tf_op jit(solution)/shard_map/pallas_call | solution.py:516
  142.9 4.1 %collective-permute-start.33 = (bf16[1024,256]{1,0:T(8,128)(2,1)S(1)}, bf16[1024,256]{1,0:T(8,128)(2,1)S(1)}, u32[]{:S(2)}, u32[]{:S(2)}) collective-permute-start(bf16[1024,256]{1,0:T(8,128)(2,1)S(1)} %get-tuple-element.110), channel_id=1, source_target_pairs={{0,112},{16,96},{32,80},{48,64},{64,48},{80,32},{96,16},{112,0},{1... | collective-permute-start | bytes 1572872 | tf_op jit(solution)/shard_map/ppermute | solution.py:568
  147.1 6.3 %shard_map.142 = (bf16[128,512]{1,0:T(8,128)(2,1)S(1)}, bf16[128,512]{1,0:T(8,128)(2,1)S(1)}, bf16[128,512]{1,0:T(8,128)(2,1)S(1)}, bf16[128,512]{1,0:T(8,128)(2...) custom-call(s32[1]{0:T(128)} %bitcast.ctx, s32[4,128]{1,0:T(4,128)S(1)} %bitcast.16, ...), custom_call_target="tpu_custom_call" | custom-call | flops 20000000000 | bytes 1048576 | tf_op jit(solution)/shard_map/pallas_call | solution.py:516
  155.1 3.3 %collective-permute-done.28.d1 = bf16[128,512]{1,0:T(8,128)(2,1)S(1)} collective-permute-done((bf16[128,512]{1,0:T(8,128)(2,1)S(1)}, bf16[128,512]{1,0:T(8,128)(2,1)S(1)}, u32[]{:S(2)}, u32[]{:S(2)}) %collective-permute-start.28) | collective-permute-done | bytes 131104 | tf_op jit(solution)/shard_map/ppermute | solution.py:568
  159.9 13.4 %collective-permute-done.29.d2 = bf16[128,512]{1,0:T(8,128)(2,1)S(1)} collective-permute-done((bf16[128,512]{1,0:T(8,128)(2,1)S(1)}, bf16[128,512]{1,0:T(8,128)(2,1)S(1)}, u32[]{:S(2)}, u32[]{:S(2)}) %collective-permute-start.29) | collective-permute-done | bytes 131104 | tf_op jit(solution)/shard_map/ppermute | solution.py:568
  (100 shorter events, 56.2 us)
Async XLA Ops:
  5.8 16.9 %collective-permute-start.3 = (bf16[1024,256]{1,0:T(8,128)(2,1)S(1)}, bf16[1024,256]{1,0:T(8,128)(2,1)S(1)}, u32[]{:S(2)}, u32[]{:S(2)}) collective-permute-start(bf16[1024,256]{1,0:T(8,128)(2,1)S(1)} %get-tuple-element.62.refs_4_.refs_5_), channel_id=1, source_target_pairs={{0,96},{16,112},{32,64},{48,80},{64,32},{80,48},{96,0},{112,16},{1... | collective-permute-start | bytes 1572872 | tf_op jit(solution)/shard_map/ppermute | solution.py:568
  8.8 8.9 %collective-permute-start = (bf16[128,512]{1,0:T(8,128)(2,1)S(1)}, bf16[128,512]{1,0:T(8,128)(2,1)S(1)}, u32[]{:S(2)}, u32[]{:S(2)}) collective-permute-start(bf16[128,512]{1,0:T(8,128)(2,1)S(1)} %get-tuple-element.60.refs_0_), channel_id=1, source_target_pairs={{0,32},{16,48},{32,0},{48,16},{64,96},{80,112},{96,64},{112,80},{1... | collective-permute-start | bytes 393224 | tf_op jit(solution)/shard_map/ppermute | solution.py:568
  9.0 11.0 %collective-permute-start.2 = (bf16[128,512]{1,0:T(8,128)(2,1)S(1)}, bf16[128,512]{1,0:T(8,128)(2,1)S(1)}, u32[]{:S(2)}, u32[]{:S(2)}) collective-permute-start(bf16[128,512]{1,0:T(8,128)(2,1)S(1)} %get-tuple-element.61), channel_id=1, source_target_pairs={{0,48},{16,32},{32,16},{48,0},{64,112},{80,96},{96,80},{112,64},{1... | collective-permute-start | bytes 393224 | tf_op jit(solution)/shard_map/ppermute | solution.py:568
  14.1 8.6 %collective-permute-start.1 = (bf16[128,512]{1,0:T(8,128)(2,1)S(1)}, bf16[128,512]{1,0:T(8,128)(2,1)S(1)}, u32[]{:S(2)}, u32[]{:S(2)}) collective-permute-start(bf16[128,512]{1,0:T(8,128)(2,1)S(1)} %get-tuple-element.61), channel_id=1, source_target_pairs={{0,16},{16,0},{32,48},{48,32},{64,80},{80,64},{96,112},{112,96},{1... | collective-permute-start | bytes 393224 | tf_op jit(solution)/shard_map/ppermute | solution.py:568
  14.1 19.2 %collective-permute-start.4 = (bf16[1024,256]{1,0:T(8,128)(2,1)S(1)}, bf16[1024,256]{1,0:T(8,128)(2,1)S(1)}, u32[]{:S(2)}, u32[]{:S(2)}) collective-permute-start(bf16[1024,256]{1,0:T(8,128)(2,1)S(1)} %get-tuple-element.66), channel_id=1, source_target_pairs={{0,16},{16,0},{32,48},{48,32},{64,80},{80,64},{96,112},{112,96},{1... | collective-permute-start | bytes 1572872 | tf_op jit(solution)/shard_map/ppermute | solution.py:568
  33.3 10.5 %collective-permute-start.5 = (bf16[512,256]{1,0:T(8,128)(2,1)S(1)}, bf16[512,256]{1,0:T(8,128)(2,1)S(1)}, u32[]{:S(2)}, u32[]{:S(2)}) collective-permute-start(bf16[512,256]{1,0:T(8,128)(2,1)S(1)} %slice.6), channel_id=1, source_target_pairs={{0,96},{16,112},{32,64},{48,80},{64,32},{80,48},{96,0},{112,16},{1... | collective-permute-start | bytes 786440 | tf_op jit(solution)/shard_map/ppermute | solution.py:568
  33.8 14.8 %collective-permute-start.6 = (bf16[512,256]{1,0:T(8,128)(2,1)S(1)}, bf16[512,256]{1,0:T(8,128)(2,1)S(1)}, u32[]{:S(2)}, u32[]{:S(2)}) collective-permute-start(bf16[512,256]{1,0:T(8,128)(2,1)S(1)} %get-tuple-element.70), channel_id=1, source_target_pairs={{0,112},{16,96},{32,80},{48,64},{64,48},{80,32},{96,16},{112,0},{1... | collective-permute-start | bytes 786440 | tf_op jit(solution)/shard_map/ppermute | solution.py:568
  40.4 19.9 %collective-permute-start.13 = (bf16[256,1024]{1,0:T(8,128)(2,1)S(1)}, bf16[256,1024]{1,0:T(8,128)(2,1)S(1)}, u32[]{:S(2)}, u32[]{:S(2)}) collective-permute-start(bf16[256,1024]{1,0:T(8,128)(2,1)S(1)} %copy-done.2), channel_id=1, source_target_pairs={{0,8},{1,9},{2,10},{3,11},{4,12},{5,13},{6,14},{7,15},{8,0},{9,1},... | collective-permute-start | bytes 1572872 | tf_op jit(solution)/shard_map/ppermute | solution.py:580
  53.6 7.3 %collective-permute-start.7 = (bf16[144,512]{1,0:T(8,128)(2,1)}, bf16[144,512]{1,0:T(8,128)(2,1)S(1)}, u32[]{:S(2)}, u32[]{:S(2)}) collective-permute-start(bf16[144,512]{1,0:T(8,128)(2,1)} %get-tuple-element.75), channel_id=1, source_target_pairs={{0,32},{16,48},{32,0},{48,16},{64,96},{80,112},{96,64},{112,80},{1... | collective-permute-start | bytes 442376 | tf_op jit(solution)/shard_map/ppermute | solution.py:568
  53.6 12.6 %collective-permute-start.8 = (bf16[144,512]{1,0:T(8,128)(2,1)}, bf16[144,512]{1,0:T(8,128)(2,1)}, u32[]{:S(2)}, u32[]{:S(2)}) collective-permute-start(bf16[144,512]{1,0:T(8,128)(2,1)} %get-tuple-element.76), channel_id=1, source_target_pairs={{0,16},{16,0},{32,48},{48,32},{64,80},{80,64},{96,112},{112,96},{1... | collective-permute-start | bytes 442376 | tf_op jit(solution)/shard_map/ppermute | solution.py:568
  55.9 10.3 %collective-permute-start.9 = (bf16[144,512]{1,0:T(8,128)(2,1)}, bf16[144,512]{1,0:T(8,128)(2,1)}, u32[]{:S(2)}, u32[]{:S(2)}) collective-permute-start(bf16[144,512]{1,0:T(8,128)(2,1)} %get-tuple-element.77), channel_id=1, source_target_pairs={{0,48},{16,32},{32,16},{48,0},{64,112},{80,96},{96,80},{112,64},{1... | collective-permute-start | bytes 442376 | tf_op jit(solution)/shard_map/ppermute | solution.py:568
  60.3 13.8 %collective-permute-start.14 = (bf16[256,1024]{1,0:T(8,128)(2,1)S(1)}, bf16[256,1024]{1,0:T(8,128)(2,1)S(1)}, u32[]{:S(2)}, u32[]{:S(2)}) collective-permute-start(bf16[256,1024]{1,0:T(8,128)(2,1)S(1)} %copy-done.2), channel_id=1, source_target_pairs={{0,1},{1,0},{2,3},{3,2},{4,5},{5,4},{6,7},{7,6},{8,9},{9,8},{10,11... | collective-permute-start | bytes 1572872 | tf_op jit(solution)/shard_map/ppermute | solution.py:580
  60.4 13.7 %collective-permute-start.15 = (bf16[256,1024]{1,0:T(8,128)(2,1)S(1)}, bf16[256,1024]{1,0:T(8,128)(2,1)S(1)}, u32[]{:S(2)}, u32[]{:S(2)}) collective-permute-start(bf16[256,1024]{1,0:T(8,128)(2,1)S(1)} %collective-permute-done.13.w2), channel_id=1, source_target_pairs={{0,1},{1,0},{2,3},{3,2},{4,5},{5,4},{6,7},{7,6},{8,9},{9,8},{10,11... | collective-permute-start | bytes 1572872 | tf_op jit(solution)/shard_map/ppermute | solution.py:580
  76.2 6.7 %collective-permute-start.17 = (bf16[32,1024]{1,0:T(8,128)(2,1)S(1)}, bf16[32,1024]{1,0:T(8,128)(2,1)S(1)}, u32[]{:S(2)}, u32[]{:S(2)}) collective-permute-start(bf16[32,1024]{1,0:T(8,128)(2,1)S(1)} %get-tuple-element.87), channel_id=1, source_target_pairs={{0,4},{1,5},{2,6},{3,7},{4,0},{5,1},{6,2},{7,3},{8,12},{9,13},{10,... | collective-permute-start | bytes 196616 | tf_op jit(solution)/shard_map/ppermute | solution.py:580
  96.5 6.2 %collective-permute-start.21 = (bf16[32,1024]{1,0:T(8,128)(2,1)S(1)}, bf16[32,1024]{1,0:T(8,128)(2,1)S(1)}, u32[]{:S(2)}, u32[]{:S(2)}) collective-permute-start(bf16[32,1024]{1,0:T(8,128)(2,1)S(1)} %get-tuple-element.89.g0), channel_id=1, source_target_pairs={{0,6},{1,7},{2,4},{3,5},{4,2},{5,3},{6,0},{7,1},{8,14},{9,15},{10,... | collective-permute-start | bytes 196616 | tf_op jit(solution)/shard_map/ppermute | solution.py:580
  97.4 5.9 %collective-permute-start.20 = (bf16[32,1024]{1,0:T(8,128)(2,1)S(1)}, bf16[32,1024]{1,0:T(8,128)(2,1)S(1)}, u32[]{:S(2)}, u32[]{:S(2)}) collective-permute-start(bf16[32,1024]{1,0:T(8,128)(2,1)S(1)} %get-tuple-element.89.g0), channel_id=1, source_target_pairs={{0,4},{1,5},{2,6},{3,7},{4,0},{5,1},{6,2},{7,3},{8,12},{9,13},{10,... | collective-permute-start | bytes 196616 | tf_op jit(solution)/shard_map/ppermute | solution.py:580
  110.4 9.2 %collective-permute-start.27 = (bf16[144,512]{1,0:T(8,128)(2,1)S(1)}, bf16[144,512]{1,0:T(8,128)(2,1)S(1)}, u32[]{:S(2)}, u32[]{:S(2)}) collective-permute-start(bf16[144,512]{1,0:T(8,128)(2,1)S(1)} %get-tuple-element.97), channel_id=1, source_target_pairs={{0,48},{16,32},{32,16},{48,0},{64,112},{80,96},{96,80},{112,64},{1... | collective-permute-start | bytes 442376 | tf_op jit(solution)/shard_map/ppermute | solution.py:568
  112.3 9.8 %collective-permute-start.26 = (bf16[144,512]{1,0:T(8,128)(2,1)S(1)}, bf16[144,512]{1,0:T(8,128)(2,1)S(1)}, u32[]{:S(2)}, u32[]{:S(2)}) collective-permute-start(bf16[144,512]{1,0:T(8,128)(2,1)S(1)} %get-tuple-element.97), channel_id=1, source_target_pairs={{0,16},{16,0},{32,48},{48,32},{64,80},{80,64},{96,112},{112,96},{1... | collective-permute-start | bytes 442376 | tf_op jit(solution)/shard_map/ppermute | solution.py:568
  113.2 8.9 %collective-permute-start.25 = (bf16[144,512]{1,0:T(8,128)(2,1)S(1)}, bf16[144,512]{1,0:T(8,128)(2,1)S(1)}, u32[]{:S(2)}, u32[]{:S(2)}) collective-permute-start(bf16[144,512]{1,0:T(8,128)(2,1)S(1)} %get-tuple-element.96.refs_1_), channel_id=1, source_target_pairs={{0,32},{16,48},{32,0},{48,16},{64,96},{80,112},{96,64},{112,80},{1... | collective-permute-start | bytes 442376 | tf_op jit(solution)/shard_map/ppermute | solution.py:568
  140.8 33.8 %collective-permute-start.31 = (bf16[1024,256]{1,0:T(8,128)(2,1)S(1)}, bf16[1024,256]{1,0:T(8,128)(2,1)S(1)}, u32[]{:S(2)}, u32[]{:S(2)}) collective-permute-start(bf16[1024,256]{1,0:T(8,128)(2,1)S(1)} %get-tuple-element.108), channel_id=1, source_target_pairs={{0,96},{16,112},{32,64},{48,80},{64,32},{80,48},{96,0},{112,16},{1... | collective-permute-start | bytes 1572872 | tf_op jit(solution)/shard_map/ppermute | solution.py:568
  141.4 33.2 %collective-permute-start.32 = (bf16[1024,256]{1,0:T(8,128)(2,1)S(1)}, bf16[1024,256]{1,0:T(8,128)(2,1)S(1)}, u32[]{:S(2)}, u32[]{:S(2)}) collective-permute-start(bf16[1024,256]{1,0:T(8,128)(2,1)S(1)} %get-tuple-element.109), channel_id=1, source_target_pairs={{0,16},{16,0},{32,48},{48,32},{64,80},{80,64},{96,112},{112,96},{1... | collective-permute-start | bytes 1572872 | tf_op jit(solution)/shard_map/ppermute | solution.py:568
  142.9 31.7 %collective-permute-start.33 = (bf16[1024,256]{1,0:T(8,128)(2,1)S(1)}, bf16[1024,256]{1,0:T(8,128)(2,1)S(1)}, u32[]{:S(2)}, u32[]{:S(2)}) collective-permute-start(bf16[1024,256]{1,0:T(8,128)(2,1)S(1)} %get-tuple-element.110), channel_id=1, source_target_pairs={{0,112},{16,96},{32,80},{48,64},{64,48},{80,32},{96,16},{112,0},{1... | collective-permute-start | bytes 1572872 | tf_op jit(solution)/shard_map/ppermute | solution.py:568
  153.4 19.9 %collective-permute-start.29 = (bf16[128,512]{1,0:T(8,128)(2,1)S(1)}, bf16[128,512]{1,0:T(8,128)(2,1)S(1)}, u32[]{:S(2)}, u32[]{:S(2)}) collective-permute-start(bf16[128,512]{1,0:T(8,128)(2,1)S(1)} %get-tuple-element.103), channel_id=1, source_target_pairs={{0,16},{16,0},{32,48},{48,32},{64,80},{80,64},{96,112},{112,96},{1... | collective-permute-start | bytes 393224 | tf_op jit(solution)/shard_map/ppermute | solution.py:568
  158.4 15.0 %collective-permute-start.30 = (bf16[128,512]{1,0:T(8,128)(2,1)S(1)}, bf16[128,512]{1,0:T(8,128)(2,1)S(1)}, u32[]{:S(2)}, u32[]{:S(2)}) collective-permute-start(bf16[128,512]{1,0:T(8,128)(2,1)S(1)} %get-tuple-element.104), channel_id=1, source_target_pairs={{0,48},{16,32},{32,16},{48,0},{64,112},{80,96},{96,80},{112,64},{1... | collective-permute-start | bytes 393224 | tf_op jit(solution)/shard_map/ppermute | solution.py:568
  (28 other events, 206.3 us)
where the time goes:
time: 178 us; the launch traced here: 177 us
  Pallas kernels  60.4 us (34%)
  waiting for transfers between devices  59.7 us (34%)
  starting transfers between devices  49.3 us (28%)
  local copies, waits for them, and re-layouts  6.52 us (4%)
    ppermute x19, waiting for transfers between devices, send_ctx(): return lax.ppermute(array, 'ctx', ctx_swap(turn, flip))  44.4 us
    ppermute x19, starting transfers between devices, send_ctx(): return lax.ppermute(array, 'ctx', ctx_swap(turn, flip))  34.5 us
    pallas_call x4, Pallas kernels, backward(): call(functools.partial(backward_kernel, blocks=blocks, starts=starts, fir...  24.9 us
    ppermute x15, waiting for transfers between devices, send_frame(): return array if mask == 0 else lax.ppermute(array, 'frame', frame_xor(mask))  15.3 us
    ppermute x15, starting transfers between devices, send_frame(): return array if mask == 0 else lax.ppermute(array, 'frame', frame_xor(mask))  14.8 us
    pallas_call x3, Pallas kernels, forward(): call(functools.partial(forward_kernel, blocks=blocks, starts=starts, firs...  13.8 us
    pallas_call x1, Pallas kernels, reward_call(): call(reward_kernel, [SMEM] + [VMEM] * 7, [((rows, vision), bf16), ((8, HD...  11.8 us
    unnamed x36, local copies, waits for them, and re-layouts  5.99 us
  transfers between devices with their start and end apart: 34, of which 19 were waited for; matrix products, arithmetic and copies ran while one was open for 0% of the time, Pallas kernels for 14%

commit v1 on v0

--- a/solution.py
+++ b/solution.py
@@ -118,28 +118,6 @@
                 head = q[:, side * HD : side * HD + HD].astype(f32)
                 turned = head * c + pltpu.roll(head, HD // 2, 1) * s
                 out[...] = turned.T.astype(bf16)
-
-
-def plan_kernel(frame, clips, frames, counts, place, live, seen):
-    slots = clips.shape[0]
-    for i in range(seen.shape[0]):
-        seen[i] = 0
-    lane = lax.broadcasted_iota(jnp.int32, place.shape, 1)
-    slot = lane // FTOK
-    total = jnp.zeros(place.shape, jnp.int32)
-    for i in range(slots):
-        clip = clips[i]
-        rank = seen[clip]
-        seen[clip] = rank + 1
-        away = clip ^ frame[0]
-        spot = (((away // 8) * 2 + away % 2) * 4 + (away // 2) % 4) * CLIP + rank
-        total = jnp.where(slot == i, spot * FTOK, total)
-
-        @pl.when(away == 0)
-        def _():
-            live[rank] = counts[frames[i]]
-
-    place[...] = total + lane % FTOK
 
 
 def fill_keys(ctx, counts, starts, kv_refs, kaug):
@@ -602,6 +580,8 @@
     query_rows = queries.shape[0]
     key_rows = keys.shape[0]
     frame_slots = query_frames.shape[0]
+    key_frames = frame_counts.shape[0]
+    in_frame = jnp.arange(FTOK, dtype=jnp.int32)
     ctx = ctx_index.reshape(1).astype(jnp.int32)
     counts = frame_counts.reshape(-1, HD)
     packed_rows = ((key_rows, 2 * HD), bf16)
@@ -627,24 +607,24 @@
     q_blocks = exchange((qs, qs, qo, qo))
     kv_par = send_ctx(kv_send, 0, 1)
 
-    place, my_counts = pl.pallas_call(
-        plan_kernel,
-        out_shape=[
-            jax.ShapeDtypeStruct((1, query_rows), jnp.int32),
-            jax.ShapeDtypeStruct((CLIP,), jnp.int32),
-        ],
-        in_specs=[SMEM] * 4,
-        out_specs=[VMEM, SMEM],
-        scratch_shapes=[pltpu.SMEM((frame_slots // CLIP,), jnp.int32)],
-        compiler_params=pltpu.CompilerParams(vmem_limit_bytes=8 * 1024 * 1024),
-    )(frame_index.reshape(1).astype(jnp.int32), clip_of_frame, query_frames, frame_counts)
-
+    slot_index = jnp.arange(frame_slots, dtype=jnp.int32)
+    same_clip = clip_of_frame[:, None] == clip_of_frame[None, :]
+    earlier = slot_index[None, :] < slot_index[:, None]
+    rank = jnp.sum(jnp.logical_and(same_clip, earlier), axis=1).astype(jnp.int32)
+    away = clip_of_frame ^ frame_index
+    quad = (away >> 3) * 2 + (away & 1)
+    slot_place = (quad * 4 + ((away >> 1) & 3)) * CLIP + rank
+    place = (slot_place[:, None] * FTOK + in_frame[None, :]).reshape(1, query_rows)
+    frame_match = query_frames[:, None] == jnp.arange(key_frames, dtype=jnp.int32)[None, :]
+    slot_counts = jnp.sum(jnp.where(frame_match, frame_counts[None, :], 0), axis=1)
+    mine = slot_place[None, :] == jnp.arange(CLIP, dtype=jnp.int32)[:, None]
+    my_counts = jnp.sum(jnp.where(mine, slot_counts[None, :], 0), axis=1).astype(jnp.int32)
+
+    kv_far_high = send_ctx(kv_high, 2, 1)
     *state, q_blocks = forward(
         ctx, counts, q_blocks, (kv_own, kv_far), ((0, 0, 1), (2, 0, 1))
     )
-    kv_high, _ = lax.optimization_barrier((kv_high, state[1]))
     kv_par, _ = lax.optimization_barrier((kv_par, state[1]))
-    kv_far_high = send_ctx(kv_high, 2, 1)
     kv_far_low = send_ctx(kv_par[:high_rows], 2, 0)
     state = forward(ctx, counts, q_blocks, (kv_par,), ((1, 0, 1),), state)
     in_proj, _ = lax.optimization_barrier((in_proj, state[1]))

time: 178 us -> 176 us (0.989)
  waiting for transfers between devices: 59.7 us -> 57.1 us
  other arithmetic: 0.01 us -> 1.95 us
    ppermute x19, waiting for transfers between devices: 44.4 us -> 40.3 us  [send_ctx(): return lax.ppermute(array, 'ctx', ctx_swap(turn, flip))]
    unnamed x36 -> x34, local copies, waits for them, and re-layouts: 5.99 us -> 5.98 us
  transfers between devices with their start and end apart: 34 -> 34, of which waited for: 19 -> 19; matrix products, arithmetic and copies ran while one was open for 0% -> 1% of each run, Pallas kernels for 14% -> 13%
where the time goes in v1:
time: 176 us; the launch traced here: 175 us
  Pallas kernels  58.7 us (33%)
  waiting for transfers between devices  57.1 us (32%)
  starting transfers between devices  50 us (28%)
  local copies, waits for them, and re-layouts  6.59 us (4%)
  other arithmetic  1.95 us (1%)
    ppermute x19, waiting for transfers between devices, send_ctx(): return lax.ppermute(array, 'ctx', ctx_swap(turn, flip))  40.3 us
    ppermute x19, starting transfers between devices, send_ctx(): return lax.ppermute(array, 'ctx', ctx_swap(turn, flip))  35.6 us
    pallas_call x4, Pallas kernels, backward(): call(functools.partial(backward_kernel, blocks=blocks, starts=starts, fir...  24.9 us
    ppermute x15, waiting for transfers between devices, send_frame(): return array if mask == 0 else lax.ppermute(array, 'frame', frame_xor(mask))  16.8 us
    ppermute x15, starting transfers between devices, send_frame(): return array if mask == 0 else lax.ppermute(array, 'frame', frame_xor(mask))  14.4 us
    pallas_call x3, Pallas kernels, forward(): call(functools.partial(forward_kernel, blocks=blocks, starts=starts, firs...  13.8 us
    pallas_call x1, Pallas kernels, reward_call(): call(reward_kernel, [SMEM] + [VMEM] * 7, [((rows, vision), bf16), ((8, HD...  11.8 us
    unnamed x34, local copies, waits for them, and re-layouts  5.98 us
  transfers between devices with their start and end apart: 34, of which 19 were waited for; matrix products, arithmetic and copies ran while one was open for 1% of the time, Pallas kernels for 13%

profile of v1, /device:TPU:0, one launch (start us, length us, event | category | flops | bytes accessed | tf_op | source)
XLA Modules:
  0.0 175.2 jit_solution(8737383944912791854)
XLA Ops:
  5.8 2.9 %collective-permute-start.3 = (bf16[1024,256]{1,0:T(8,128)(2,1)S(1)}, bf16[1024,256]{1,0:T(8,128)(2,1)S(1)}, u32[]{:S(2)}, u32[]{:S(2)}) collective-permute-start(bf16[1024,256]{1,0:T(8,128)(2,1)S(1)} %get-tuple-element.59.refs_4_.refs_5_), channel_id=1, source_target_pairs={{0,96},{16,112},{32,64},{48,80},{64,32},{80,48},{96,0},{112,16},{1... | collective-permute-start | bytes 1572872 | tf_op jit(solution)/shard_map/ppermute | solution.py:546
  8.8 3.5 %collective-permute-start.2 = (bf16[128,512]{1,0:T(8,128)(2,1)S(1)}, bf16[128,512]{1,0:T(8,128)(2,1)S(1)}, u32[]{:S(2)}, u32[]{:S(2)}) collective-permute-start(bf16[128,512]{1,0:T(8,128)(2,1)S(1)} %get-tuple-element.58), channel_id=1, source_target_pairs={{0,48},{16,32},{32,16},{48,0},{64,112},{80,96},{96,80},{112,64},{1... | collective-permute-start | bytes 393224 | tf_op jit(solution)/shard_map/ppermute | solution.py:546
  14.1 3.4 %collective-permute-start.6 = (bf16[512,256]{1,0:T(8,128)(2,1)S(1)}, bf16[512,256]{1,0:T(8,128)(2,1)S(1)}, u32[]{:S(2)}, u32[]{:S(2)}) collective-permute-start(bf16[512,256]{1,0:T(8,128)(2,1)S(1)} %get-tuple-element.64), channel_id=1, source_target_pairs={{0,112},{16,96},{32,80},{48,64},{64,48},{80,32},{96,16},{112,0},{1... | collective-permute-start | bytes 786440 | tf_op jit(solution)/shard_map/ppermute | solution.py:546
  22.5 6.0 %shard_map.130 = (f32[4,128,512]{2,1,0:T(8,128)S(1)}, f32[4,8,512]{2,1,0:T(8,128)S(1)}, bf16[4,256,512]{2,1,0:T(8,128)(2,1)S(1)}) custom-call(s32[1]{0:T(128)} %bitcast.ctx, s32[4,128]{1,0:T(4,128)S(1)} %bitcast.9, bf16[128,512]{1,0:T(8,128)(2,1)S(1)} %get-tuple-element.57.refs_0_, bf16[128,512]{1,0:T(8,128)(2,1)S(1)} %collective-permute-done.refs_1_, ...), custom_call_target="tpu_custom_call" | custom-call | flops 10000000000 | bytes 1048576 | tf_op jit(solution)/shard_map/pallas_call | solution.py:237
  28.5 11.1 %collective-permute-done.4.refs_1_.refs_5_ = bf16[1024,256]{1,0:T(8,128)(2,1)S(1)} collective-permute-done((bf16[1024,256]{1,0:T(8,128)(2,1)S(1)}, bf16[1024,256]{1,0:T(8,128)(2,1)S(1)}, u32[]{:S(2)}, u32[]{:S(2)}) %collective-permute-start.4) | collective-permute-done | bytes 524320 | tf_op jit(solution)/shard_map/ppermute | solution.py:546
  41.5 3.5 %shard_map.131 = (f32[4,128,512]{2,1,0:T(8,128)S(1)}, f32[4,8,512]{2,1,0:T(8,128)S(1)}) custom-call(s32[1]{0:T(128)} %bitcast.ctx, s32[4,128]{1,0:T(4,128)S(1)} %bitcast.10, bf16[4,256,512]{2,1,0:T(8,128)(2,1)S(1)} %get-tuple-element.60.refs_0_, bf16[1024,256]{1,0:T(8,128)(2,1)S(1)} %collective-permute-done.4.refs_1_.refs_5_, ...), custom_call_target="tpu_custom_call" | custom-call | flops 10000000000 | bytes 1048576 | tf_op jit(solution)/shard_map/pallas_call | solution.py:237
  48.0 4.3 %shard_map.132 = (bf16[144,512]{1,0:T(8,128)(2,1)S(1)}, bf16[144,512]{1,0:T(8,128)(2,1)}, bf16[144,512]{1,0:T(8,128)(2,1)}, bf16[144,512]{1,0:T(8,128)(2,1)}) custom-call(s32[1]{0:T(128)} %bitcast.ctx, s32[4,128]{1,0:T(4,128)S(1)} %bitcast.11, bf16[4,256,512]{2,1,0:T(8,128)(2,1)S(1)} %get-tuple-element.60.refs_0_, ...), custom_call_target="tpu_custom_call" | custom-call | flops 10000000000 | bytes 1048576 | tf_op jit(solution)/shard_map/pallas_call | solution.py:237
  53.9 4.0 %collective-permute-start.9 = (bf16[144,512]{1,0:T(8,128)(2,1)}, bf16[144,512]{1,0:T(8,128)(2,1)}, u32[]{:S(2)}, u32[]{:S(2)}) collective-permute-start(bf16[144,512]{1,0:T(8,128)(2,1)} %get-tuple-element.71), channel_id=1, source_target_pairs={{0,48},{16,32},{32,16},{48,0},{64,112},{80,96},{96,80},{112,64},{1... | collective-permute-start | bytes 442376 | tf_op jit(solution)/shard_map/ppermute | solution.py:546
  60.5 2.9 %collective-permute-done.8.refs_2_ = bf16[144,512]{1,0:T(8,128)(2,1)} collective-permute-done((bf16[144,512]{1,0:T(8,128)(2,1)}, bf16[144,512]{1,0:T(8,128)(2,1)}, u32[]{:S(2)}, u32[]{:S(2)}) %collective-permute-start.8) | collective-permute-done | bytes 147488 | tf_op jit(solution)/shard_map/ppermute | solution.py:546
  68.0 3.0 %collective-permute-done.11.o2 = bf16[128,256]{1,0:T(8,128)(2,1)S(1)} collective-permute-done((bf16[128,256]{1,0:T(8,128)(2,1)S(1)}, bf16[128,256]{1,0:T(8,128)(2,1)S(1)}, u32[]{:S(2)}, u32[]{:S(2)}) %collective-permute-start.11) | collective-permute-done | bytes 65568 | tf_op jit(solution)/shard_map/ppermute | solution.py:558
  73.5 2.9 %collective-permute-start.17 = (bf16[32,1024]{1,0:T(8,128)(2,1)S(1)}, bf16[32,1024]{1,0:T(8,128)(2,1)S(1)}, u32[]{:S(2)}, u32[]{:S(2)}) collective-permute-start(bf16[32,1024]{1,0:T(8,128)(2,1)S(1)} %get-tuple-element.81), channel_id=1, source_target_pairs={{0,4},{1,5},{2,6},{3,7},{4,0},{5,1},{6,2},{7,3},{8,12},{9,13},{10,... | collective-permute-start | bytes 196616 | tf_op jit(solution)/shard_map/ppermute | solution.py:558
  76.7 3.4 %collective-permute-done.17.x2 = bf16[32,1024]{1,0:T(8,128)(2,1)S(1)} collective-permute-done((bf16[32,1024]{1,0:T(8,128)(2,1)S(1)}, bf16[32,1024]{1,0:T(8,128)(2,1)S(1)}, u32[]{:S(2)}, u32[]{:S(2)}) %collective-permute-start.17) | collective-permute-done | bytes 65568 | tf_op jit(solution)/shard_map/ppermute | solution.py:558
  81.9 11.8 %shard_map.135 = (bf16[32,1024]{1,0:T(8,128)(2,1)S(1)}, f32[8,128]{1,0:T(8,128)S(1)}) custom-call(s32[2]{0:T(128)S(1)} %fusion.1.counts, f32[32,1024]{1,0:T(8,128)S(1)} %get-tuple-element.79.x0, bf16[32,1024]{1,0:T(8,128)(2,1)S(1)} %collective-permute-done.16.x1, bf16[32,1024]{1,0:T(8,128)(2,1)S(1)} %collective-permute-done.17.x2, ...), custom_call_target="tpu_custom_call" | custom-call | bytes 1048576 | tf_op jit(solution)/shard_map/pallas_call | solution.py:372
  103.6 3.2 %collective-permute-done.23.d2 = bf16[128,256]{1,0:T(8,128)(2,1)S(1)} collective-permute-done((bf16[128,256]{1,0:T(8,128)(2,1)S(1)}, bf16[128,256]{1,0:T(8,128)(2,1)S(1)}, u32[]{:S(2)}, u32[]{:S(2)}) %collective-permute-start.23) | collective-permute-done | bytes 65568 | tf_op jit(solution)/shard_map/ppermute | solution.py:558
  107.5 3.2 %collective-permute-start.27 = (bf16[144,512]{1,0:T(8,128)(2,1)S(1)}, bf16[144,512]{1,0:T(8,128)(2,1)S(1)}, u32[]{:S(2)}, u32[]{:S(2)}) collective-permute-start(bf16[144,512]{1,0:T(8,128)(2,1)S(1)} %get-tuple-element.91), channel_id=1, source_target_pairs={{0,48},{16,32},{32,16},{48,0},{64,112},{80,96},{96,80},{112,64},{1... | collective-permute-start | bytes 442376 | tf_op jit(solution)/shard_map/ppermute | solution.py:546
  112.6 3.8 %collective-permute-done.27.refs_4_ = bf16[144,512]{1,0:T(8,128)(2,1)S(1)} collective-permute-done((bf16[144,512]{1,0:T(8,128)(2,1)S(1)}, bf16[144,512]{1,0:T(8,128)(2,1)S(1)}, u32[]{:S(2)}, u32[]{:S(2)}) %collective-permute-start.27) | collective-permute-done | bytes 147488 | tf_op jit(solution)/shard_map/ppermute | solution.py:546
  116.5 2.9 %collective-permute-done.26.refs_3_ = bf16[144,512]{1,0:T(8,128)(2,1)S(1)} collective-permute-done((bf16[144,512]{1,0:T(8,128)(2,1)S(1)}, bf16[144,512]{1,0:T(8,128)(2,1)S(1)}, u32[]{:S(2)}, u32[]{:S(2)}) %collective-permute-start.26) | collective-permute-done | bytes 147488 | tf_op jit(solution)/shard_map/ppermute | solution.py:546
  119.3 6.2 %shard_map.138 = (f32[4,128,512]{2,1,0:T(8,128)S(1)}, bf16[1024,256]{1,0:T(8,128)(2,1)S(1)}) custom-call(s32[1]{0:T(128)} %bitcast.ctx, s32[4,128]{1,0:T(4,128)S(1)} %bitcast.12, bf16[4,256,512]{2,1,0:T(8,128)(2,1)S(1)} %copy-done.10, bf16[144,512]{1,0:T(8,128)(2,1)S(1)} %get-tuple-element.90.refs_1_, bf16[144,512]{1,0:T(8,128)(2,1)S(1)} %collective-permute-done.25.refs_2_, ...), custom_call_target="tpu_custom_call" | custom-call | flops 20000000000 | bytes 1048576 | tf_op jit(solution)/shard_map/pallas_call | solution.py:494
  125.6 6.2 %shard_map.139 = (f32[4,128,512]{2,1,0:T(8,128)S(1)}, bf16[1024,256]{1,0:T(8,128)(2,1)S(1)}) custom-call(s32[1]{0:T(128)} %bitcast.ctx, s32[4,128]{1,0:T(4,128)S(1)} %bitcast.13, bf16[4,256,512]{2,1,0:T(8,128)(2,1)S(1)} %copy-done.10, bf16[144,512]{1,0:T(8,128)(2,1)S(1)} %get-tuple-element.90.refs_1_, bf16[144,512]{1,0:T(8,128)(2,1)S(1)} %collective-permute-done.25.refs_2_, ...), custom_call_target="tpu_custom_call" | custom-call | flops 20000000000 | bytes 1048576 | tf_op jit(solution)/shard_map/pallas_call | solution.py:494
  131.8 6.2 %shard_map.140 = (f32[4,128,512]{2,1,0:T(8,128)S(1)}, bf16[1024,256]{1,0:T(8,128)(2,1)S(1)}) custom-call(s32[1]{0:T(128)} %bitcast.ctx, s32[4,128]{1,0:T(4,128)S(1)} %bitcast.14, bf16[4,256,512]{2,1,0:T(8,128)(2,1)S(1)} %copy-done.10, bf16[144,512]{1,0:T(8,128)(2,1)S(1)} %get-tuple-element.90.refs_1_, bf16[144,512]{1,0:T(8,128)(2,1)S(1)} %collective-permute-done.25.refs_2_, ...), custom_call_target="tpu_custom_call" | custom-call | flops 20000000000 | bytes 1048576 | tf_op jit(solution)/shard_map/pallas_call | solution.py:494
  140.1 2.9 %collective-permute-start.32 = (bf16[1024,256]{1,0:T(8,128)(2,1)S(1)}, bf16[1024,256]{1,0:T(8,128)(2,1)S(1)}, u32[]{:S(2)}, u32[]{:S(2)}) collective-permute-start(bf16[1024,256]{1,0:T(8,128)(2,1)S(1)} %get-tuple-element.103), channel_id=1, source_target_pairs={{0,16},{16,0},{32,48},{48,32},{64,80},{80,64},{96,112},{112,96},{1... | collective-permute-start | bytes 1572872 | tf_op jit(solution)/shard_map/ppermute | solution.py:546
  144.3 6.3 %shard_map.141 = (bf16[128,512]{1,0:T(8,128)(2,1)S(1)}, bf16[128,512]{1,0:T(8,128)(2,1)S(1)}, bf16[128,512]{1,0:T(8,128)(2,1)S(1)}, bf16[128,512]{1,0:T(8,128)(2...) custom-call(s32[1]{0:T(128)} %bitcast.ctx, s32[4,128]{1,0:T(4,128)S(1)} %bitcast.15, ...), custom_call_target="tpu_custom_call" | custom-call | flops 20000000000 | bytes 1048576 | tf_op jit(solution)/shard_map/pallas_call | solution.py:494
  150.6 2.7 %collective-permute-start.29 = (bf16[128,512]{1,0:T(8,128)(2,1)S(1)}, bf16[128,512]{1,0:T(8,128)(2,1)S(1)}, u32[]{:S(2)}, u32[]{:S(2)}) collective-permute-start(bf16[128,512]{1,0:T(8,128)(2,1)S(1)} %get-tuple-element.97), channel_id=1, source_target_pairs={{0,16},{16,0},{32,48},{48,32},{64,80},{80,64},{96,112},{112,96},{1... | collective-permute-start | bytes 393224 | tf_op jit(solution)/shard_map/ppermute | solution.py:546
  158.1 13.7 %collective-permute-done.29.d2 = bf16[128,512]{1,0:T(8,128)(2,1)S(1)} collective-permute-done((bf16[128,512]{1,0:T(8,128)(2,1)S(1)}, bf16[128,512]{1,0:T(8,128)(2,1)S(1)}, u32[]{:S(2)}, u32[]{:S(2)}) %collective-permute-start.29) | collective-permute-done | bytes 131104 | tf_op jit(solution)/shard_map/ppermute | solution.py:546
  (103 shorter events, 54.2 us)
Async XLA Ops:
  5.8 16.0 %collective-permute-start.3 = (bf16[1024,256]{1,0:T(8,128)(2,1)S(1)}, bf16[1024,256]{1,0:T(8,128)(2,1)S(1)}, u32[]{:S(2)}, u32[]{:S(2)}) collective-permute-start(bf16[1024,256]{1,0:T(8,128)(2,1)S(1)} %get-tuple-element.59.refs_4_.refs_5_), channel_id=1, source_target_pairs={{0,96},{16,112},{32,64},{48,80},{64,32},{80,48},{96,0},{112,16},{1... | collective-permute-start | bytes 1572872 | tf_op jit(solution)/shard_map/ppermute | solution.py:546
  8.8 12.0 %collective-permute-start.2 = (bf16[128,512]{1,0:T(8,128)(2,1)S(1)}, bf16[128,512]{1,0:T(8,128)(2,1)S(1)}, u32[]{:S(2)}, u32[]{:S(2)}) collective-permute-start(bf16[128,512]{1,0:T(8,128)(2,1)S(1)} %get-tuple-element.58), channel_id=1, source_target_pairs={{0,48},{16,32},{32,16},{48,0},{64,112},{80,96},{96,80},{112,64},{1... | collective-permute-start | bytes 393224 | tf_op jit(solution)/shard_map/ppermute | solution.py:546
  12.3 8.5 %collective-permute-start.1 = (bf16[128,512]{1,0:T(8,128)(2,1)S(1)}, bf16[128,512]{1,0:T(8,128)(2,1)S(1)}, u32[]{:S(2)}, u32[]{:S(2)}) collective-permute-start(bf16[128,512]{1,0:T(8,128)(2,1)S(1)} %get-tuple-element.58), channel_id=1, source_target_pairs={{0,16},{16,0},{32,48},{48,32},{64,80},{80,64},{96,112},{112,96},{1... | collective-permute-start | bytes 393224 | tf_op jit(solution)/shard_map/ppermute | solution.py:546
  12.6 7.2 %collective-permute-start = (bf16[128,512]{1,0:T(8,128)(2,1)S(1)}, bf16[128,512]{1,0:T(8,128)(2,1)S(1)}, u32[]{:S(2)}, u32[]{:S(2)}) collective-permute-start(bf16[128,512]{1,0:T(8,128)(2,1)S(1)} %get-tuple-element.57.refs_0_), channel_id=1, source_target_pairs={{0,32},{16,48},{32,0},{48,16},{64,96},{80,112},{96,64},{112,80},{1... | collective-permute-start | bytes 393224 | tf_op jit(solution)/shard_map/ppermute | solution.py:546
  14.1 32.0 %collective-permute-start.6 = (bf16[512,256]{1,0:T(8,128)(2,1)S(1)}, bf16[512,256]{1,0:T(8,128)(2,1)S(1)}, u32[]{:S(2)}, u32[]{:S(2)}) collective-permute-start(bf16[512,256]{1,0:T(8,128)(2,1)S(1)} %get-tuple-element.64), channel_id=1, source_target_pairs={{0,112},{16,96},{32,80},{48,64},{64,48},{80,32},{96,16},{112,0},{1... | collective-permute-start | bytes 786440 | tf_op jit(solution)/shard_map/ppermute | solution.py:546
  19.9 19.7 %collective-permute-start.4 = (bf16[1024,256]{1,0:T(8,128)(2,1)S(1)}, bf16[1024,256]{1,0:T(8,128)(2,1)S(1)}, u32[]{:S(2)}, u32[]{:S(2)}) collective-permute-start(bf16[1024,256]{1,0:T(8,128)(2,1)S(1)} %get-tuple-element.61), channel_id=1, source_target_pairs={{0,16},{16,0},{32,48},{48,32},{64,80},{80,64},{96,112},{112,96},{1... | collective-permute-start | bytes 1572872 | tf_op jit(solution)/shard_map/ppermute | solution.py:546
  39.6 8.3 %collective-permute-start.5 = (bf16[512,256]{1,0:T(8,128)(2,1)S(1)}, bf16[512,256]{1,0:T(8,128)(2,1)S(1)}, u32[]{:S(2)}, u32[]{:S(2)}) collective-permute-start(bf16[512,256]{1,0:T(8,128)(2,1)S(1)} %slice.6), channel_id=1, source_target_pairs={{0,96},{16,112},{32,64},{48,80},{64,32},{80,48},{96,0},{112,16},{1... | collective-permute-start | bytes 786440 | tf_op jit(solution)/shard_map/ppermute | solution.py:546
  45.0 15.0 %collective-permute-start.13 = (bf16[256,1024]{1,0:T(8,128)(2,1)S(1)}, bf16[256,1024]{1,0:T(8,128)(2,1)S(1)}, u32[]{:S(2)}, u32[]{:S(2)}) collective-permute-start(bf16[256,1024]{1,0:T(8,128)(2,1)S(1)} %copy-done.2), channel_id=1, source_target_pairs={{0,8},{1,9},{2,10},{3,11},{4,12},{5,13},{6,14},{7,15},{8,0},{9,1},... | collective-permute-start | bytes 1572872 | tf_op jit(solution)/shard_map/ppermute | solution.py:558
  52.9 7.6 %collective-permute-start.7 = (bf16[144,512]{1,0:T(8,128)(2,1)}, bf16[144,512]{1,0:T(8,128)(2,1)S(1)}, u32[]{:S(2)}, u32[]{:S(2)}) collective-permute-start(bf16[144,512]{1,0:T(8,128)(2,1)} %get-tuple-element.69), channel_id=1, source_target_pairs={{0,32},{16,48},{32,0},{48,16},{64,96},{80,112},{96,64},{112,80},{1... | collective-permute-start | bytes 442376 | tf_op jit(solution)/shard_map/ppermute | solution.py:546
  52.9 10.5 %collective-permute-start.8 = (bf16[144,512]{1,0:T(8,128)(2,1)}, bf16[144,512]{1,0:T(8,128)(2,1)}, u32[]{:S(2)}, u32[]{:S(2)}) collective-permute-start(bf16[144,512]{1,0:T(8,128)(2,1)} %get-tuple-element.70), channel_id=1, source_target_pairs={{0,16},{16,0},{32,48},{48,32},{64,80},{80,64},{96,112},{112,96},{1... | collective-permute-start | bytes 442376 | tf_op jit(solution)/shard_map/ppermute | solution.py:546
  53.9 9.5 %collective-permute-start.9 = (bf16[144,512]{1,0:T(8,128)(2,1)}, bf16[144,512]{1,0:T(8,128)(2,1)}, u32[]{:S(2)}, u32[]{:S(2)}) collective-permute-start(bf16[144,512]{1,0:T(8,128)(2,1)} %get-tuple-element.71), channel_id=1, source_target_pairs={{0,48},{16,32},{32,16},{48,0},{64,112},{80,96},{96,80},{112,64},{1... | collective-permute-start | bytes 442376 | tf_op jit(solution)/shard_map/ppermute | solution.py:546
  60.0 11.3 %collective-permute-start.14 = (bf16[256,1024]{1,0:T(8,128)(2,1)S(1)}, bf16[256,1024]{1,0:T(8,128)(2,1)S(1)}, u32[]{:S(2)}, u32[]{:S(2)}) collective-permute-start(bf16[256,1024]{1,0:T(8,128)(2,1)S(1)} %copy-done.2), channel_id=1, source_target_pairs={{0,1},{1,0},{2,3},{3,2},{4,5},{5,4},{6,7},{7,6},{8,9},{9,8},{10,11... | collective-permute-start | bytes 1572872 | tf_op jit(solution)/shard_map/ppermute | solution.py:558
  60.0 11.3 %collective-permute-start.15 = (bf16[256,1024]{1,0:T(8,128)(2,1)S(1)}, bf16[256,1024]{1,0:T(8,128)(2,1)S(1)}, u32[]{:S(2)}, u32[]{:S(2)}) collective-permute-start(bf16[256,1024]{1,0:T(8,128)(2,1)S(1)} %collective-permute-done.13.w2), channel_id=1, source_target_pairs={{0,1},{1,0},{2,3},{3,2},{4,5},{5,4},{6,7},{7,6},{8,9},{9,8},{10,11... | collective-permute-start | bytes 1572872 | tf_op jit(solution)/shard_map/ppermute | solution.py:558
  73.5 6.7 %collective-permute-start.17 = (bf16[32,1024]{1,0:T(8,128)(2,1)S(1)}, bf16[32,1024]{1,0:T(8,128)(2,1)S(1)}, u32[]{:S(2)}, u32[]{:S(2)}) collective-permute-start(bf16[32,1024]{1,0:T(8,128)(2,1)S(1)} %get-tuple-element.81), channel_id=1, source_target_pairs={{0,4},{1,5},{2,6},{3,7},{4,0},{5,1},{6,2},{7,3},{8,12},{9,13},{10,... | collective-permute-start | bytes 196616 | tf_op jit(solution)/shard_map/ppermute | solution.py:558
  93.7 6.2 %collective-permute-start.21 = (bf16[32,1024]{1,0:T(8,128)(2,1)S(1)}, bf16[32,1024]{1,0:T(8,128)(2,1)S(1)}, u32[]{:S(2)}, u32[]{:S(2)}) collective-permute-start(bf16[32,1024]{1,0:T(8,128)(2,1)S(1)} %get-tuple-element.83.g0), channel_id=1, source_target_pairs={{0,6},{1,7},{2,4},{3,5},{4,2},{5,3},{6,0},{7,1},{8,14},{9,15},{10,... | collective-permute-start | bytes 196616 | tf_op jit(solution)/shard_map/ppermute | solution.py:558
  94.6 5.9 %collective-permute-start.20 = (bf16[32,1024]{1,0:T(8,128)(2,1)S(1)}, bf16[32,1024]{1,0:T(8,128)(2,1)S(1)}, u32[]{:S(2)}, u32[]{:S(2)}) collective-permute-start(bf16[32,1024]{1,0:T(8,128)(2,1)S(1)} %get-tuple-element.83.g0), channel_id=1, source_target_pairs={{0,4},{1,5},{2,6},{3,7},{4,0},{5,1},{6,2},{7,3},{8,12},{9,13},{10,... | collective-permute-start | bytes 196616 | tf_op jit(solution)/shard_map/ppermute | solution.py:558
  107.5 8.9 %collective-permute-start.27 = (bf16[144,512]{1,0:T(8,128)(2,1)S(1)}, bf16[144,512]{1,0:T(8,128)(2,1)S(1)}, u32[]{:S(2)}, u32[]{:S(2)}) collective-permute-start(bf16[144,512]{1,0:T(8,128)(2,1)S(1)} %get-tuple-element.91), channel_id=1, source_target_pairs={{0,48},{16,32},{32,16},{48,0},{64,112},{80,96},{96,80},{112,64},{1... | collective-permute-start | bytes 442376 | tf_op jit(solution)/shard_map/ppermute | solution.py:546
  110.7 8.6 %collective-permute-start.26 = (bf16[144,512]{1,0:T(8,128)(2,1)S(1)}, bf16[144,512]{1,0:T(8,128)(2,1)S(1)}, u32[]{:S(2)}, u32[]{:S(2)}) collective-permute-start(bf16[144,512]{1,0:T(8,128)(2,1)S(1)} %get-tuple-element.91), channel_id=1, source_target_pairs={{0,16},{16,0},{32,48},{48,32},{64,80},{80,64},{96,112},{112,96},{1... | collective-permute-start | bytes 442376 | tf_op jit(solution)/shard_map/ppermute | solution.py:546
  111.4 7.9 %collective-permute-start.25 = (bf16[144,512]{1,0:T(8,128)(2,1)S(1)}, bf16[144,512]{1,0:T(8,128)(2,1)S(1)}, u32[]{:S(2)}, u32[]{:S(2)}) collective-permute-start(bf16[144,512]{1,0:T(8,128)(2,1)S(1)} %get-tuple-element.90.refs_1_), channel_id=1, source_target_pairs={{0,32},{16,48},{32,0},{48,16},{64,96},{80,112},{96,64},{112,80},{1... | collective-permute-start | bytes 442376 | tf_op jit(solution)/shard_map/ppermute | solution.py:546
  138.0 35.1 %collective-permute-start.31 = (bf16[1024,256]{1,0:T(8,128)(2,1)S(1)}, bf16[1024,256]{1,0:T(8,128)(2,1)S(1)}, u32[]{:S(2)}, u32[]{:S(2)}) collective-permute-start(bf16[1024,256]{1,0:T(8,128)(2,1)S(1)} %get-tuple-element.102), channel_id=1, source_target_pairs={{0,96},{16,112},{32,64},{48,80},{64,32},{80,48},{96,0},{112,16},{1... | collective-permute-start | bytes 1572872 | tf_op jit(solution)/shard_map/ppermute | solution.py:546
  140.1 33.0 %collective-permute-start.32 = (bf16[1024,256]{1,0:T(8,128)(2,1)S(1)}, bf16[1024,256]{1,0:T(8,128)(2,1)S(1)}, u32[]{:S(2)}, u32[]{:S(2)}) collective-permute-start(bf16[1024,256]{1,0:T(8,128)(2,1)S(1)} %get-tuple-element.103), channel_id=1, source_target_pairs={{0,16},{16,0},{32,48},{48,32},{64,80},{80,64},{96,112},{112,96},{1... | collective-permute-start | bytes 1572872 | tf_op jit(solution)/shard_map/ppermute | solution.py:546
  143.0 30.1 %collective-permute-start.33 = (bf16[1024,256]{1,0:T(8,128)(2,1)S(1)}, bf16[1024,256]{1,0:T(8,128)(2,1)S(1)}, u32[]{:S(2)}, u32[]{:S(2)}) collective-permute-start(bf16[1024,256]{1,0:T(8,128)(2,1)S(1)} %get-tuple-element.104), channel_id=1, source_target_pairs={{0,112},{16,96},{32,80},{48,64},{64,48},{80,32},{96,16},{112,0},{1... | collective-permute-start | bytes 1572872 | tf_op jit(solution)/shard_map/ppermute | solution.py:546
  150.6 21.2 %collective-permute-start.29 = (bf16[128,512]{1,0:T(8,128)(2,1)S(1)}, bf16[128,512]{1,0:T(8,128)(2,1)S(1)}, u32[]{:S(2)}, u32[]{:S(2)}) collective-permute-start(bf16[128,512]{1,0:T(8,128)(2,1)S(1)} %get-tuple-element.97), channel_id=1, source_target_pairs={{0,16},{16,0},{32,48},{48,32},{64,80},{80,64},{96,112},{112,96},{1... | collective-permute-start | bytes 393224 | tf_op jit(solution)/shard_map/ppermute | solution.py:546
  155.6 16.2 %collective-permute-start.30 = (bf16[128,512]{1,0:T(8,128)(2,1)S(1)}, bf16[128,512]{1,0:T(8,128)(2,1)S(1)}, u32[]{:S(2)}, u32[]{:S(2)}) collective-permute-start(bf16[128,512]{1,0:T(8,128)(2,1)S(1)} %get-tuple-element.98), channel_id=1, source_target_pairs={{0,48},{16,32},{32,16},{48,0},{64,112},{80,96},{96,80},{112,64},{1... | collective-permute-start | bytes 393224 | tf_op jit(solution)/shard_map/ppermute | solution.py:546
  (27 other events, 193.4 us)
